TPU v7x, 256 devices: a whole 4x4x8 slice. The times are simulated.
256 devices in a mesh: tile: 64 (over z, x, core), mem: 4 (over y).
Axes of the slice: x: 4, y: 4, z: 8, core: 2. Of those that a mesh axis runs over, the one named last changes fastest.
Arguments:
- footprints: bfloat16 [8192, 128, 128], P('tile'), may hold values from -0.1875 to 0.1875
- tile_row: int32 [8192], P('tile'), may hold values from 0 to 1023, as said below
- tile_col: int32 [8192], P('tile'), may hold values from 0 to 511, as said below
- prior_flux: bfloat16 [256, 65536], P('mem', 'tile'), may hold values from -12 to 12
- observed: float32 [256, 131072], P('mem', 'tile'), may hold values from -6 to 6
- precision_weight: int32 [131072], P('tile'), may hold values from 1 to 16
Outputs:
- gradient: float32 [256, 65536], P('mem', 'tile')
Inputs may be any that keep to these rules, and one draw needn't show every extreme that they name: Among the 128 tiles of each index of tile, at most 3 have a row block of one owner (owner = tile_row // 16); in every draw one owner gets exactly 3 from every index. Likewise with owner = tile_col // 8: at most 3 from one index of tile to one owner, and one owner gets exactly 3 from every index.
All inputs are finite; a program needn't handle non-finite values.
Results may differ from a plain program's by a relative error of at most 0.0052.
Values may be sent and summed in bfloat16 or wider, within the bound.
A program may use at most 64 MiB of HBM per device.

v0:
```python
import jax
import jax.numpy as jnp
from jax import lax
from jax.sharding import PartitionSpec as P

MEMBERS = 256
FLUX_DEV = 8
SOUND_DEV = 16


def sent_to_all(value, axis):
    size = lax.axis_size(axis)
    return lax.all_to_all(
        jnp.broadcast_to(value[None], (size, *value.shape)), axis, 0, 0, tiled=True
    )


def over_copies(value, axis):
    return sent_to_all(value, axis).sum(axis=0)


def slot_of(owners, capacity):
    entries = owners.shape[0]
    position = jnp.arange(entries)
    earlier = (owners[:, None] == owners[None, :]) & (position[None, :] < position[:, None])
    return owners * capacity + jnp.sum(earlier.astype(jnp.int32), axis=1)


def invert(slot_ids, slot_total):
    matches = slot_ids[None, :] == jnp.arange(slot_total)[:, None]
    sources = jnp.sum(jnp.where(matches, jnp.arange(slot_ids.shape[0])[None, :], 0), axis=1)
    return (sources, jnp.any(matches, axis=1))


def to_slots(values, sources, usage_flags):
    placed = jnp.take(values, sources, axis=1)
    return jnp.where(usage_flags[None, :, None], placed, jnp.zeros_like(placed))


def body(footprints, tile_row, tile_col, prior_flux, observed, precision_weight):
    devices_tile = lax.axis_size("tile")
    tile_count = footprints.shape[0]
    tile_size = footprints.shape[1]
    capacity = tile_count // devices_tile + max(1, tile_count // (2 * devices_tile))
    slot_total = devices_tile * capacity
    local_members = prior_flux.shape[0]
    local_sum = jnp.sum(prior_flux.astype(jnp.float32), axis=0)
    ensemble_sum = over_copies(local_sum, "mem")
    ensemble_mean = ensemble_sum / MEMBERS
    member_deviations = (prior_flux.astype(jnp.float32) - ensemble_mean[None, :]).astype(
        jnp.bfloat16
    )
    row_owner = tile_row // SOUND_DEV
    row_local = tile_row % SOUND_DEV
    col_owner = tile_col // FLUX_DEV
    col_local = tile_col % FLUX_DEV
    row_slot = slot_of(row_owner, capacity)
    col_slot = slot_of(col_owner, capacity)
    row_source, row_used = invert(row_slot, slot_total)
    col_source, col_used = invert(col_slot, slot_total)
    gathered = lax.all_gather(member_deviations, "tile", axis=1, tiled=True)
    retrieved_blocks = jnp.take(gathered.reshape(local_members, -1, tile_size), tile_col, axis=1)
    forward_terms = jnp.einsum(
        "mtk,trk->mtr", retrieved_blocks, footprints, preferred_element_type=jnp.float32
    )
    row_index = jnp.where(row_used, jnp.take(row_local, row_source), SOUND_DEV)
    sent_terms = to_slots(forward_terms, row_source, row_used)
    got_terms, got_rows = (
        lax.all_to_all(
            sent_terms.astype(jnp.bfloat16), "tile", split_axis=1, concat_axis=1, tiled=True
        ).astype(sent_terms.dtype),
        lax.all_to_all(row_index[None, :], "tile", split_axis=1, concat_axis=1, tiled=True),
    )
    got_rows = got_rows[0]
    row_match = (got_rows[None, :] == jnp.arange(SOUND_DEV)[:, None]).astype(jnp.float32)
    modelled = jnp.einsum("ds,msk->mdk", row_match, got_terms, precision=lax.Precision.HIGHEST)
    targets = observed.reshape(local_members, SOUND_DEV, tile_size)
    obs_weight = (precision_weight.astype(jnp.float32) / 8.0).reshape(SOUND_DEV, tile_size)
    weighted = (obs_weight[None, :, :] * (modelled - targets)).astype(jnp.bfloat16)
    reply_rows = jnp.take(weighted, jnp.minimum(got_rows, SOUND_DEV - 1), axis=1)
    returned = lax.all_to_all(reply_rows, "tile", split_axis=1, concat_axis=1, tiled=True)
    residual_tiles = jnp.take(returned, row_slot, axis=1)
    backward_terms = jnp.einsum(
        "mtr,trk->mtk", residual_tiles, footprints, preferred_element_type=jnp.float32
    )
    col_index = jnp.where(col_used, jnp.take(col_local, col_source), FLUX_DEV)
    sent_back = to_slots(backward_terms, col_source, col_used)
    got_back, got_cols = (
        lax.all_to_all(
            sent_back.astype(jnp.bfloat16), "tile", split_axis=1, concat_axis=1, tiled=True
        ).astype(sent_back.dtype),
        lax.all_to_all(col_index[None, :], "tile", split_axis=1, concat_axis=1, tiled=True),
    )
    col_match = (got_cols[0][None, :] == jnp.arange(FLUX_DEV)[:, None]).astype(jnp.float32)
    reduced_total = jnp.einsum("fs,msk->mfk", col_match, got_back, precision=lax.Precision.HIGHEST)
    gradient = reduced_total.reshape(local_members, FLUX_DEV * tile_size)
    return gradient


def solution(mesh):
    in_specs = (
        P("tile", None, None),
        P("tile"),
        P("tile"),
        P("mem", "tile"),
        P("mem", "tile"),
        P("tile"),
    )
    out_specs = P("mem", "tile")
    return jax.shard_map(body, mesh=mesh, in_specs=in_specs, out_specs=out_specs, check_vma=False)
```

profile of v0, /device:TPU:8, one launch (start us, length us, event | category | flops | bytes accessed | tf_op | source)
XLA Modules:
  0.0 407.8 jit_solution(12967651325447050244)
XLA Ops:
  6.5 0.0 all-gather.2.cloned.1.call-start
  6.5 0.9 convert_reduce_fusion
  7.5 8.6 %all_to_all.39 = f32[4,1,1024]{2,1,0:T(1,128)S(1)} all-to-all(f32[4,1,1024]{2,1,0:T(1,128)S(1)} %broadcast_in_dim.122), channel_id=1, replica_groups=mesh['tile'=64,'mem'=4] {'mem'}, dimensions={0} | all-to-all | bytes 32768 | tf_op jit(solution)/shard_map/all_to_all | solution.py:13
  16.1 1.6 fusion.26
  17.7 0.0 all-gather.2.cloned.1.call-update
  17.8 0.7 and_select_fusion.1
  18.4 0.2 convert_reduce_fusion.1
  18.6 0.1 select_reduce_fusion.1
  18.8 1.6 gather_fusion.3
  20.3 0.1 fusion.27
  20.4 0.7 all_to_all.25
  21.2 11.9 %all-to-all-start = ((s32[1,64,3]{2,0,1:T(1,128)}), s32[1,64,3]{2,0,1:T(1,128)S(1)}, u32[]{:S(2)}, u32[]{:S(2)}) async-start(s32[1,64,3]{2,0,1:T(1,128)} %bitcast), calls=%async_computation | async-start | bytes 65536 | tf_op jit(solution)/shard_map/all_to_all | solution.py:72
  33.1 0.7 and_select_fusion
  33.8 0.7 compare_and_fusion.2
  34.5 68.2 %all-gather.2.cloned.1.call-done = bf16[64,65536]{1,0:T(8,128)(2,1)} async-done(((bf16[64,1024]{1,0:T(8,128)(2,1)}), bf16[64,65536]{1,0:T(8,128)(2,1)}) %all-gather.2.cloned.1.call-update) | async-done | bytes 8388624 | tf_op jit(solution)/shard_map/all_gather | solution.py:61
  102.7 9.0 %copy_bitcast_fusion = bf16[64,512,128]{2,0,1:T(8,128)(2,1)} fusion(bf16[64,65536]{1,0:T(8,128)(2,1)} %all-gather.2.cloned.1.call-done), kind=kLoop, calls=%fused_computation.7 | loop fusion | bytes 16777216 | tf_op jit(solution)/shard_map/reshape | solution.py:62
  111.7 5.5 %gather_fusion = bf16[128,64,128]{2,1,0:T(8,128)(2,1)} fusion(bf16[64,512,128]{2,0,1:T(8,128)(2,1)} %copy_bitcast_fusion, s32[1024]{0:T(1024)S(1)} %pad_clamp_fusion.3), kind=kCustom, calls=%fused_computation.4 | custom fusion | bytes 4194816 | tf_op jit(solution)/shard_map/jit(_take)/gather | solution.py:62
  117.3 5.8 %convolution_bitcast_fusion.1 = bf16[64,128,128]{2,0,1:T(8,128)(2,1)S(1)} fusion(bf16[128,128,128]{2,1,0:T(8,128)(2,1)} %param.10, bf16[128,64,128]{2,1,0:T(8,128)(2,1)} %gather_fusion, pred[128]{0:T(512)(128)(4,1)S(1)} %compare_and_fusion.2), kind=kOutput, calls=%fused_computation.18 | convolution fusion | flops 269484032 | bytes 8388736 | tf_op jit(solution)/shard_map/mtk,trk->mtr/dot_general | solution.py:63
  123.0 2.7 gather_fusion.4
  125.7 4.3 %fusion.1 = bf16[64,192,128]{2,0,1:T(8,128)(2,1)} fusion(bf16[192,64,128]{2,1,0:T(8,128)(2,1)} %gather_fusion.4, pred[192]{0:T(512)(128)(4,1)S(1)} %get-tuple-element.14, pred[192]{0:T(512)(128)(4,1)S(1)} %fusion.27), kind=kLoop, calls=%fused_computation.11 | loop fusion | flops 3145728 | bytes 6291840 | tf_op jit(solution)/shard_map/convert_element_type | solution.py:70
  130.0 0.0 copy-start
  130.0 0.0 all-to-all-done
  130.0 6.5 %all-to-all-start.2 = ((bf16[64,192,128]{2,0,1:T(8,128)(2,1)}), bf16[64,192,128]{2,0,1:T(8,128)(2,1)S(1)}, u32[]{:S(2)}, u32[]{:S(2)}) async-start(bf16[64,192,128]{2,0,1:T(8,128)(2,1)} %fusion.1), calls=%async_computation.2 | async-start | bytes 6291456 | tf_op jit(solution)/shard_map/all_to_all | solution.py:69
  136.5 1.9 copy.34
  138.4 0.0 copy-done
  138.4 0.5 broadcast.195
  139.0 0.7 minimum_reduce_fusion
  139.7 0.1 squeeze.3
  139.8 0.1 min.26
  140.0 70.4 %all-to-all-done.2 = bf16[64,192,128]{2,0,1:T(8,128)(2,1)S(1)} async-done(((bf16[64,192,128]{2,0,1:T(8,128)(2,1)}), bf16[64,192,128]{2,0,1:T(8,128)(2,1)S(1)}, u32[]{:S(2)}, u32[]{:S(2)}) %all-to-all-start.2) | async-done | bytes 3145760 | tf_op jit(solution)/shard_map/all_to_all | solution.py:69
  210.4 2.8 fusion.21
  213.2 0.1 copy.29
  213.3 1.2 gather_fusion.1
  214.5 2.1 select_bitcast_fusion
  216.5 5.3 %all-to-all-start.3 = ((bf16[64,192,128]{2,0,1:T(8,128)(2,1)}), bf16[64,192,128]{2,0,1:T(8,128)(2,1)S(1)}, u32[]{:S(2)}, u32[]{:S(2)}) async-start(bf16[64,192,128]{2,0,1:T(8,128)(2,1)} %select_bitcast_fusion), calls=%async_computation.3 | async-start | bytes 6291456 | tf_op jit(solution)/shard_map/all_to_all | solution.py:81
  221.8 0.2 convert_reduce_fusion.2
  222.0 0.1 select_reduce_fusion
  222.2 1.6 gather_fusion.6
  223.7 0.1 fusion.28
  223.9 0.8 all_to_all.31
  224.6 71.1 %all-to-all-done.3 = bf16[64,192,128]{2,0,1:T(8,128)(2,1)S(1)} async-done(((bf16[64,192,128]{2,0,1:T(8,128)(2,1)}), bf16[64,192,128]{2,0,1:T(8,128)(2,1)S(1)}, u32[]{:S(2)}, u32[]{:S(2)}) %all-to-all-start.3) | async-done | bytes 3145760 | tf_op jit(solution)/shard_map/all_to_all | solution.py:81
  295.7 5.3 %all-to-all-start.5 = ((s32[1,64,3]{2,0,1:T(1,128)}), s32[1,64,3]{2,0,1:T(1,128)S(1)}, u32[]{:S(2)}, u32[]{:S(2)}) async-start(s32[1,64,3]{2,0,1:T(1,128)} %bitcast.12), calls=%async_computation.5 | async-start | bytes 65536 | tf_op jit(solution)/shard_map/all_to_all | solution.py:92
  301.0 2.2 gather_fusion.2
  303.2 4.1 %convolution_bitcast_fusion = bf16[64,128,128]{2,0,1:T(8,128)(2,1)S(1)} fusion(bf16[128,128,128]{2,1,0:T(8,128)(2,1)} %param.10, bf16[128,64,128]{2,1,0:T(8,128)(2,1)} %gather_fusion.2, pred[128]{0:T(512)(128)(4,1)S(1)} %get-tuple-element.11), kind=kOutput, calls=%fused_computation.17 | convolution fusion | flops 269484032 | bytes 8388736 | tf_op jit(solution)/shard_map/mtr,trk->mtk/dot_general | solution.py:83
  307.3 2.7 gather_fusion.5
  310.0 4.3 %fusion = bf16[64,192,128]{2,0,1:T(8,128)(2,1)} fusion(bf16[192,64,128]{2,1,0:T(8,128)(2,1)} %gather_fusion.5, pred[192]{0:T(512)(128)(4,1)S(1)} %get-tuple-element.10, pred[192]{0:T(512)(128)(4,1)S(1)} %fusion.28), kind=kLoop, calls=%fused_computation.9 | loop fusion | flops 3145728 | bytes 6291840 | tf_op jit(solution)/shard_map/convert_element_type | solution.py:90
  314.3 0.0 all-to-all-done.5
  314.3 10.3 %all-to-all-start.4 = ((bf16[64,192,128]{2,0,1:T(8,128)(2,1)}), bf16[64,192,128]{2,0,1:T(8,128)(2,1)S(1)}, u32[]{:S(2)}, u32[]{:S(2)}) async-start(bf16[64,192,128]{2,0,1:T(8,128)(2,1)} %fusion), calls=%async_computation.4 | async-start | bytes 6291456 | tf_op jit(solution)/shard_map/all_to_all | solution.py:89
  324.6 0.6 reduce.12
  325.2 0.1 eq.98
  325.4 73.1 %all-to-all-done.4 = bf16[64,192,128]{2,0,1:T(8,128)(2,1)S(1)} async-done(((bf16[64,192,128]{2,0,1:T(8,128)(2,1)}), bf16[64,192,128]{2,0,1:T(8,128)(2,1)S(1)}, u32[]{:S(2)}, u32[]{:S(2)}) %all-to-all-start.4) | async-done | bytes 3145760 | tf_op jit(solution)/shard_map/all_to_all | solution.py:89
  398.5 1.7 fusion.2
  400.2 0.8 copy.50
  (18 shorter events, 0.1 us)
Async XLA Ops:
  6.5 96.2 %all-gather.2.cloned.1.call-start = ((), (), s32[]{:S(2)}) async-start(), calls=%async_computation.6 | async-start | bytes 8519680 | tf_op jit(solution)/shard_map/all_gather | solution.py:61
  21.2 108.8 %all-to-all-start = ((s32[1,64,3]{2,0,1:T(1,128)}), s32[1,64,3]{2,0,1:T(1,128)S(1)}, u32[]{:S(2)}, u32[]{:S(2)}) async-start(s32[1,64,3]{2,0,1:T(1,128)} %bitcast), calls=%async_computation | async-start | bytes 65536 | tf_op jit(solution)/shard_map/all_to_all | solution.py:72
  130.0 8.4 %copy-start = (s32[2048]{0:T(1024)S(1)}, s32[2048]{0:T(1024)}, u32[]{:S(2)}) copy-start(s32[2048]{0:T(1024)} %param.15) | copy-start | bytes 24580
  130.0 80.4 %all-to-all-start.2 = ((bf16[64,192,128]{2,0,1:T(8,128)(2,1)}), bf16[64,192,128]{2,0,1:T(8,128)(2,1)S(1)}, u32[]{:S(2)}, u32[]{:S(2)}) async-start(bf16[64,192,128]{2,0,1:T(8,128)(2,1)} %fusion.1), calls=%async_computation.2 | async-start | bytes 6291456 | tf_op jit(solution)/shard_map/all_to_all | solution.py:69
  216.5 79.2 %all-to-all-start.3 = ((bf16[64,192,128]{2,0,1:T(8,128)(2,1)}), bf16[64,192,128]{2,0,1:T(8,128)(2,1)S(1)}, u32[]{:S(2)}, u32[]{:S(2)}) async-start(bf16[64,192,128]{2,0,1:T(8,128)(2,1)} %select_bitcast_fusion), calls=%async_computation.3 | async-start | bytes 6291456 | tf_op jit(solution)/shard_map/all_to_all | solution.py:81
  295.7 18.6 %all-to-all-start.5 = ((s32[1,64,3]{2,0,1:T(1,128)}), s32[1,64,3]{2,0,1:T(1,128)S(1)}, u32[]{:S(2)}, u32[]{:S(2)}) async-start(s32[1,64,3]{2,0,1:T(1,128)} %bitcast.12), calls=%async_computation.5 | async-start | bytes 65536 | tf_op jit(solution)/shard_map/all_to_all | solution.py:92
  314.3 84.2 %all-to-all-start.4 = ((bf16[64,192,128]{2,0,1:T(8,128)(2,1)}), bf16[64,192,128]{2,0,1:T(8,128)(2,1)S(1)}, u32[]{:S(2)}, u32[]{:S(2)}) async-start(bf16[64,192,128]{2,0,1:T(8,128)(2,1)} %fusion), calls=%async_computation.4 | async-start | bytes 6291456 | tf_op jit(solution)/shard_map/all_to_all | solution.py:89
Sparse Core Ops, SparseCore 0:
  17.9 84.7 all-gather.1
where the time goes:
time: 409 us; the launch traced here: 408 us
  waiting for transfers between devices  283 us (69%)
  starting transfers between devices  39.3 us (10%)
  local copies, waits for them, and re-layouts  31.6 us (8%)
  other arithmetic  17.4 us (4%)
  matrix products  14.4 us (4%)
  between operations  13.6 us (3%)
  blocking collectives  8.61 us (2%)
    all_to_all x1, waiting for transfers between devices, body(): lax.all_to_all(sent_back.astype(jnp.bfloat16), 'tile', split_axis=1, conc...  73.1 us
    all_to_all x1, waiting for transfers between devices, body(): lax.all_to_all(reply_rows, 'tile', split_axis=1, concat_axis=1, tiled=True)  71.1 us
    all_to_all x1, waiting for transfers between devices, body(): lax.all_to_all(sent_terms.astype(jnp.bfloat16), 'tile', split_axis=1, con...  70.4 us
    all_gather x1, waiting for transfers between devices, body(): gathered = lax.all_gather(member_deviations, 'tile', axis=1, tiled=True)  68.2 us
    all_to_all x1, starting transfers between devices, body(): lax.all_to_all(row_index[None, :], 'tile', split_axis=1, concat_axis=1, t...  11.9 us
    all_to_all x1, starting transfers between devices, body(): lax.all_to_all(sent_back.astype(jnp.bfloat16), 'tile', split_axis=1, conc...  10.3 us
    reshape x1, local copies, waits for them, and re-layouts, body(): gathered.reshape(local_members, -1, tile_size)  9.01 us
    all_to_all x1, blocking collectives, sent_to_all(): lax.all_to_all(jnp.broadcast_to(value[None], (size, *value.shape)), axis,...  8.61 us
  transfers between devices with their start and end apart: 6, of which 4 were waited for; matrix products, arithmetic and copies ran while one was open for 12% of the time, Pallas kernels for 0%

commit v1 on v0

v1 whole, which is shorter than its diff:
```python
import functools

import jax
import jax.numpy as jnp
from jax import lax
from jax.experimental import pallas as pl
from jax.experimental.pallas import tpu as pltpu
from jax.sharding import PartitionSpec as P

MEMBERS = 256
FLUX_DEV = 8
SOUND_DEV = 16
NZ, NX, NY, NT = 8, 4, 4, 64
CAP = 3
B = 128
LM = 64
MESH = pl.DeviceIdType.MESH
F32, BF16 = jnp.float32, jnp.bfloat16


def route(tile_row, tile_col):
    count = tile_row.shape[0]
    owner = tile_row // SOUND_DEV
    position = jnp.arange(count)
    earlier = (owner[:, None] == owner[None, :]) & (position[None, :] < position[:, None])
    slot = owner * CAP + jnp.sum(earlier.astype(jnp.int32), axis=1)
    match = slot[None, :] == jnp.arange(NT * CAP)[:, None]
    source = jnp.sum(jnp.where(match, position[None, :], 0), axis=1)
    blocks = (tile_row % SOUND_DEV) * 512 + tile_col
    coded = jnp.sum(jnp.where(match, blocks[None, :] + 1, 0), axis=1)
    coded = jnp.where(coded == 0, SOUND_DEV * 512, coded - 1)
    coded = jnp.pad(coded.reshape(NT, CAP), ((0, 0), (0, B - CAP))).reshape(NT, 1, B)
    return source, coded


def spread_kernel(
    source, coded, footprints, prior, tiles, anoms, codes,
    quarter, staged, sums, shard,
    s_fp, s_sum, r_sum, s_tile, r_tile, s_code, r_code, s_y, r_y, r_y2,
    s_local, s_z, r_z, s_x, r_x, r_x2, s_sib, r_sib,
):
    me = lax.axis_index("tile")
    q = lax.axis_index("mem")
    core = lax.rem(me, 2)
    x = lax.rem(me // 2, NX)
    z = me // 8

    def at_z(o):
        return lax.rem(z + o + NZ, NZ)

    def at_x(o):
        return lax.rem(x + o + NX, NX)

    def at_y(o):
        return lax.rem(q + o + NY, NY)

    def index(zz, xx, cc):
        return zz * 8 + xx * 2 + cc

    def remote(src, dst, ssem, rsem, tile=None, mem=None):
        return pltpu.make_async_remote_copy(
            src_ref=src, dst_ref=dst, send_sem=ssem, recv_sem=rsem,
            device_id={"tile": me if tile is None else tile, "mem": q if mem is None else mem},
            device_id_type=MESH,
        )

    def wait_for(ref, sem):
        pltpu.make_async_copy(ref, ref, sem).wait()

    fp_copy = pltpu.make_async_copy(
        footprints.at[:, pl.ds(pl.multiple_of(q * 32, 32), 32), :], quarter, s_fp
    )
    fp_copy.start()

    barrier = pltpu.get_barrier_semaphore()

    @pl.loop(1, NT)
    def _(o):
        pl.semaphore_signal(
            barrier, inc=1, device_id={"tile": lax.rem(me + o, NT), "mem": q}, device_id_type=MESH
        )

    for o in range(1, NY):
        pl.semaphore_signal(
            barrier, inc=1, device_id={"tile": me, "mem": at_y(o)}, device_id_type=MESH
        )

    for j in range(FLUX_DEV):
        part = jnp.sum(prior[:, j * B : (j + 1) * B].astype(F32), axis=0, keepdims=True)
        sums[0, j : j + 1, :] = part
    pl.semaphore_wait(barrier, NT - 1 + NY - 1)

    sum_sends = []
    for o in range(1, NY):
        cp = remote(sums.at[0], sums.at[o], s_sum.at[o], r_sum.at[o], mem=at_y(o))
        cp.start()
        sum_sends.append(cp)
    fp_copy.wait()

    def send_tiles(dz):
        first = 1 if dz == 0 else 0

        @pl.loop(first, 8)
        def _(o):
            t = at_z(dz) * 8 + lax.rem(me + o, 8)
            for s in range(CAP):
                staged[t, s] = quarter[source[t * CAP + s]]
            remote(staged.at[t], tiles.at[q, me], s_tile, r_tile.at[dz], tile=t).start()
            remote(coded.at[t], codes.at[me], s_code, r_code, tile=t).start()

        if dz == 0:
            for s in range(CAP):
                staged[me, s] = quarter[source[me * CAP + s]]
            pltpu.make_async_copy(staged.at[me], tiles.at[q, me], r_tile.at[0]).start()
            pltpu.make_async_copy(coded.at[me], codes.at[me], r_code).start()

    def group(quarter_index, dz, first=0, size=8):
        zs = at_z(-dz)
        return tiles.at[quarter_index, pl.ds(zs * 8 + first, size)]

    pending = []

    def go(cp):
        cp.start()
        pending.append(cp)

    def y_first(dz):
        wait_for(group(q, dz), r_tile.at[dz])
        go(remote(group(q, dz), group(q, dz), s_y.at[0, dz], r_y.at[0, dz], mem=at_y(1)))
        go(remote(group(q, dz), group(q, dz), s_y.at[1, dz], r_y.at[1, dz], mem=at_y(-1)))

    def y_second(dz):
        back = group(at_y(-1), dz)
        wait_for(back, r_y.at[0, dz])
        part = group(at_y(-1), dz, 0, 4)
        go(remote(part, part, s_y.at[2, dz], r_y2.at[0, dz], mem=at_y(1)))
        fore = group(at_y(1), dz)
        wait_for(fore, r_y.at[1, dz])
        part = group(at_y(1), dz, 4, 4)
        go(remote(part, part, s_y.at[3, dz], r_y2.at[1, dz], mem=at_y(-1)))

    def y_last(dz):
        wait_for(group(at_y(2), dz, 0, 4), r_y2.at[0, dz])
        wait_for(group(at_y(2), dz, 4, 4), r_y2.at[1, dz])

    def block(oz, ox, own_core=True):
        return anoms.at[index(at_z(oz), at_x(ox), core if own_core else 1 - core)]

    def to_sibling(oz, ox):
        go(
            remote(
                block(oz, ox), block(oz, ox), s_sib.at[ox % NX, oz % NZ], r_sib.at[ox % NX, oz % NZ],
                tile=index(z, x, 1 - core),
            )
        )

    def x_first(oz, src=None):
        b = block(oz, 0)
        src = b if src is None else src
        k = oz % NZ
        go(remote(src, b, s_x.at[0, k], r_x.at[0, k], tile=index(z, at_x(1), core)))
        go(remote(src, b, s_x.at[1, k], r_x.at[1, k], tile=index(z, at_x(-1), core)))
        go(remote(src, b, s_sib.at[0, k], r_sib.at[0, k], tile=index(z, x, 1 - core)))

    def x_second(oz):
        k = oz % NZ
        b = block(oz, -1)
        wait_for(b, r_x.at[0, k])
        h = b.at[pl.ds(0, 4)]
        go(remote(h, h, s_x.at[2, k], r_x2.at[0, k], tile=index(z, at_x(1), core)))
        to_sibling(oz, -1)
        b = block(oz, 1)
        wait_for(b, r_x.at[1, k])
        h = b.at[pl.ds(4, 4)]
        go(remote(h, h, s_x.at[3, k], r_x2.at[1, k], tile=index(z, at_x(-1), core)))
        to_sibling(oz, 1)

    def x_last(oz):
        k = oz % NZ
        b = block(oz, 2)
        wait_for(b.at[pl.ds(0, 4)], r_x2.at[0, k])
        wait_for(b.at[pl.ds(4, 4)], r_x2.at[1, k])
        to_sibling(oz, 2)

    def z_step(k):
        up, down = index(at_z(1), x, core), index(at_z(-1), x, core)
        if k < 4:
            b = block(-k, 0)
            wait_for(b, r_z.at[0, k])
            h = b if k < 3 else b.at[pl.ds(0, 4)]
            go(remote(h, h, s_z.at[0, k + 1], r_z.at[0, k + 1], tile=up))
            x_first(-k)
            b = block(k, 0)
            wait_for(b, r_z.at[1, k])
            h = b if k < 3 else b.at[pl.ds(4, 4)]
            go(remote(h, h, s_z.at[1, k + 1], r_z.at[1, k + 1], tile=down))
            x_first(k)
        else:
            b = block(4, 0)
            wait_for(b.at[pl.ds(0, 4)], r_z.at[0, 4])
            wait_for(b.at[pl.ds(4, 4)], r_z.at[1, 4])
            x_first(4)

    send_tiles(0)

    for cp in sum_sends:
        cp.wait()
    mean = (sums[0] + sums[1] + sums[2] + sums[3]) / MEMBERS
    for j in range(FLUX_DEV):
        shard[j] = (prior[:, j * B : (j + 1) * B].astype(F32) - mean[j : j + 1, :]).astype(BF16)
    own_copy = pltpu.make_async_copy(shard, anoms.at[me], s_local)
    own_copy.start()
    go(remote(shard, anoms.at[me], s_z.at[0, 1], r_z.at[0, 1], tile=index(at_z(1), x, core)))
    go(remote(shard, anoms.at[me], s_z.at[1, 1], r_z.at[1, 1], tile=index(at_z(-1), x, core)))
    x_first(0, shard)

    send_tiles(1)
    send_tiles(7)
    y_first(0)
    z_step(1)
    send_tiles(2)
    send_tiles(6)
    x_second(0)
    y_first(1)
    y_first(7)
    z_step(2)
    send_tiles(3)
    send_tiles(5)
    y_second(0)
    x_second(-1)
    x_second(1)
    z_step(3)
    send_tiles(4)
    y_second(1)
    y_second(7)
    y_first(2)
    y_first(6)
    x_last(0)
    x_second(-2)
    x_second(2)
    z_step(4)
    y_first(3)
    y_first(5)
    y_second(2)
    y_second(6)
    x_last(-1)
    x_last(1)
    x_second(-3)
    x_second(3)
    y_first(4)
    y_second(3)
    y_second(5)
    x_last(-2)
    x_last(2)
    x_second(4)
    y_second(4)
    x_last(-3)
    x_last(3)
    x_last(4)
    for dz in (0, 1, 7, 2, 6, 3, 5, 4):
        y_last(dz)
    for oz in (0, 1, 7, 2, 6, 3, 5, 4):
        for ox in range(NX):
            wait_for(block(oz, ox, False), r_sib.at[ox, oz])
    wait_for(codes, r_code)
    own_copy.wait()
    for cp in pending:
        cp.wait_send()
    wait_for(staged.at[pl.ds(0, NT - 1)], s_tile)
    wait_for(codes.at[pl.ds(0, NT - 1)], s_code)


def spread(source, coded, footprints, prior):
    any_spec = pl.BlockSpec(memory_space=pl.ANY)
    vmem = pl.BlockSpec(memory_space=pltpu.VMEM)
    dma = pltpu.SemaphoreType.DMA
    return pl.pallas_call(
        spread_kernel,
        out_shape=(
            jax.ShapeDtypeStruct((NY, NT, CAP, 32, B), BF16),
            jax.ShapeDtypeStruct((NT, FLUX_DEV, LM, B), BF16),
            jax.ShapeDtypeStruct((NT, 1, B), jnp.int32),
        ),
        in_specs=[pl.BlockSpec(memory_space=pltpu.SMEM), vmem, any_spec, vmem],
        out_specs=(any_spec, any_spec, any_spec),
        scratch_shapes=[
            pltpu.VMEM((B, 32, B), BF16),
            pltpu.VMEM((NT, CAP, 32, B), BF16),
            pltpu.VMEM((NY, FLUX_DEV, B), F32),
            pltpu.VMEM((FLUX_DEV, LM, B), BF16),
            dma, dma((NY,)), dma((NY,)), dma, dma((NZ,)), dma, dma,
            dma((4, NZ)), dma((2, NZ)), dma((2, NZ)),
            dma, dma((2, 5)), dma((2, 5)), dma((4, NZ)), dma((2, NZ)), dma((2, NZ)),
            dma((NX, NZ)), dma((NX, NZ)),
        ],
        compiler_params=pltpu.CompilerParams(
            collective_id=0, has_side_effects=True, vmem_limit_bytes=16 * 2**20
        ),
        name="spread",
    )(source, coded, footprints, prior)


def local_kernel(
    codes, tiles_h, anoms_h, observed, weight, out_h,
    tiles, anoms, modelled, weighted, total, packed, s_tiles, s_anoms, s_out,
):
    anoms_in = pltpu.make_async_copy(anoms_h, anoms, s_anoms)
    anoms_in.start()
    tiles_in = pltpu.make_async_copy(tiles_h, tiles, s_tiles)
    tiles_in.start()
    modelled[...] = jnp.zeros_like(modelled)

    @pl.loop(0, 64)
    def _(i):
        total[pl.ds(i * 8, 8)] = jnp.zeros((8, LM, B), F32)

    anoms_in.wait()
    tiles_in.wait()
    step = 2

    def fetch(i, o, s):
        src = i * step + o
        code = codes[src, 0, s]
        return tiles[:, src, s].reshape(B, B), code // 512, lax.rem(code, 512)

    @pl.loop(0, NT // step)
    def _(i):
        terms = []
        for o in range(step):
            for s in range(CAP):
                tile, row, col = fetch(i, o, s)
                term = lax.dot_general(
                    anoms[col], tile, (((1,), (1,)), ((), ())), preferred_element_type=F32
                )
                terms.append((row, term))
        for row, term in terms:
            modelled[row] += term

    for r in range(SOUND_DEV):
        factor = weight[r].astype(F32) / 8.0
        gap = modelled[r] - observed[:, r * B : (r + 1) * B]
        weighted[r] = (factor * gap).astype(BF16)
    weighted[SOUND_DEV] = jnp.zeros((LM, B), BF16)

    @pl.loop(0, NT // step)
    def _(i):
        terms = []
        for o in range(step):
            for s in range(CAP):
                tile, row, col = fetch(i, o, s)
                term = lax.dot_general(
                    weighted[row], tile, (((1,), (0,)), ((), ())), preferred_element_type=F32
                )
                terms.append((col, term))
        for col, term in terms:
            total[col] += term

    @pl.loop(0, 8)
    def _(i):
        @pl.loop(0, 8)
        def _(j):
            packed[pl.ds((i * 8 + j) * 8, 8)] = total[pl.ds((i * 8 + j) * 8, 8)].astype(BF16)

        pltpu.make_async_copy(
            packed.at[pl.ds(i * 64, 64)], out_h.at[pl.ds(i * 64, 64)], s_out
        ).start()

    pltpu.make_async_copy(packed, out_h, s_out).wait()


def local(codes, tiles, anoms, observed, weight):
    any_spec = pl.BlockSpec(memory_space=pl.ANY)
    vmem = pl.BlockSpec(memory_space=pltpu.VMEM)
    dma = pltpu.SemaphoreType.DMA
    return pl.pallas_call(
        local_kernel,
        out_shape=jax.ShapeDtypeStruct((NT * FLUX_DEV, LM, B), BF16),
        in_specs=[pl.BlockSpec(memory_space=pltpu.SMEM), any_spec, any_spec, vmem, vmem],
        out_specs=any_spec,
        scratch_shapes=[
            pltpu.VMEM((NY, NT, CAP, 32, B), BF16),
            pltpu.VMEM((NT * FLUX_DEV, LM, B), BF16),
            pltpu.VMEM((SOUND_DEV + 1, LM, B), F32),
            pltpu.VMEM((SOUND_DEV + 1, LM, B), BF16),
            pltpu.VMEM((NT * FLUX_DEV, LM, B), F32),
            pltpu.VMEM((NT * FLUX_DEV, LM, B), BF16),
            dma, dma, dma,
        ],
        compiler_params=pltpu.CompilerParams(vmem_limit_bytes=50 * 2**20),
        name="local",
    )(codes, tiles, anoms.reshape(NT * FLUX_DEV, LM, B), observed, weight)


def gather_kernel(
    part, out,
    pa, pb, ra, rb, xa1, xa2, zb1, zb2, za1, za2, xb1, xb2,
    s_own_a, s_own_b, s_sib_a, r_sib_a, s_sib_b, r_sib_b,
    s_xa, r_xa, s_zb, r_zb, s_za, r_za, s_xb, r_xb,
):
    me = lax.axis_index("tile")
    q = lax.axis_index("mem")
    core = lax.rem(me, 2)
    x = lax.rem(me // 2, NX)
    z = me // 8

    def at_z(o):
        return lax.rem(z + o + NZ, NZ)

    def at_x(o):
        return lax.rem(x + o + NX, NX)

    def index(zz, xx, cc):
        return zz * 8 + xx * 2 + cc

    sibling = index(z, x, 1 - core)
    x_next = (index(z, at_x(1), core), index(z, at_x(-1), core))
    z_next = (index(at_z(1), x, core), index(at_z(-1), x, core))

    pending = []

    def send(src, dst, ssem, rsem, tile):
        cp = pltpu.make_async_remote_copy(
            src_ref=src, dst_ref=dst, send_sem=ssem, recv_sem=rsem,
            device_id={"tile": tile, "mem": q}, device_id_type=MESH,
        )
        cp.start()
        pending.append(cp)

    def wait_for(ref, sem):
        pltpu.make_async_copy(ref, ref, sem).wait()

    def own(kind, d):
        if kind == "a":
            return part.at[:, at_x(d), core, pl.ds(0, 4)], pa.at[d], s_own_a.at[d]
        return part.at[at_z(d), :, core, pl.ds(4, 4)], pb.at[d], s_own_b.at[d]

    order = [("a", 2), ("b", 4), ("b", 3), ("b", 5), ("a", 1), ("a", 3),
             ("b", 2), ("b", 6), ("b", 1), ("b", 7), ("b", 0), ("a", 0)]
    for kind, d in order:
        pltpu.make_async_copy(*own(kind, d)).start()

    barrier = pltpu.get_barrier_semaphore()
    for t in (sibling, *x_next, *z_next):
        pl.semaphore_signal(barrier, inc=1, device_id={"tile": t, "mem": q}, device_id_type=MESH)
    pl.semaphore_wait(barrier, 5)

    for kind, d in order:
        if kind == "a":
            send(part.at[:, at_x(d), 1 - core, pl.ds(0, 4)], ra.at[d], s_sib_a.at[d], r_sib_a.at[d], sibling)
        else:
            send(part.at[at_z(d), :, 1 - core, pl.ds(4, 4)], rb.at[d], s_sib_b.at[d], r_sib_b.at[d], sibling)

    def add(dst, *srcs):
        @pl.loop(0, dst.shape[0])
        def _(i):
            for b in range(dst.shape[1]):
                value = dst[i, b].astype(F32)
                for s in srcs:
                    value = value + s[i, b].astype(F32)
                dst[i, b] = value.astype(BF16)

    def settle(kind, d):
        pltpu.make_async_copy(*own(kind, d)).wait()
        if kind == "a":
            wait_for(ra.at[d], r_sib_a.at[d])
        else:
            wait_for(rb.at[d], r_sib_b.at[d])

    def pair(kind, d):
        settle(kind, d)
        if kind == "a":
            add(pa.at[d], ra.at[d])
        else:
            add(pb.at[d], rb.at[d])

    pair("a", 2)
    for i in range(2):
        send(pa.at[2, pl.ds(4 * i, 4)], xa1.at[i], s_xa.at[i, 0], r_xa.at[i, 0], x_next[i])
    pair("b", 4)
    for i in range(2):
        send(pb.at[4, pl.ds(2 * i, 2)], zb1.at[i], s_zb.at[i, 0], r_zb.at[i, 0], z_next[i])
    pair("b", 3)
    pair("b", 5)
    for i, d in enumerate((3, 5)):
        wait_for(zb1.at[i], r_zb.at[i, 0])
        add(pb.at[d, pl.ds(2 * i, 2)], zb1.at[i])
        send(pb.at[d], zb2.at[i, 0], s_zb.at[i, 1], r_zb.at[i, 1], z_next[i])
    pair("a", 1)
    pair("a", 3)
    for i, d in enumerate((1, 3)):
        wait_for(xa1.at[i], r_xa.at[i, 0])
        add(pa.at[d, pl.ds(4 * i, 4)], xa1.at[i])
        send(pa.at[d], xa2.at[i], s_xa.at[i, 1], r_xa.at[i, 1], x_next[i])
    for step in (1, 2):
        pair("b", 3 - step)
        pair("b", 5 + step)
        for i, d in enumerate((3 - step, 5 + step)):
            wait_for(zb2.at[i, step - 1], r_zb.at[i, step])
            add(pb.at[d], zb2.at[i, step - 1])
            send(pb.at[d], zb2.at[i, step], s_zb.at[i, step + 1], r_zb.at[i, step + 1], z_next[i])

    settle("a", 0)
    for i in range(2):
        wait_for(xa2.at[i], r_xa.at[i, 1])
    add(pa.at[0], ra.at[0], xa2.at[0], xa2.at[1])
    for i in range(2):
        send(pa.at[0, at_z(4), pl.ds(2 * i, 2)], za1.at[i], s_za.at[i, 0], r_za.at[i, 0], z_next[i])

    def add3(dst, src):
        for b in range(dst.shape[0]):
            dst[b] = (dst[b].astype(F32) + src[b].astype(F32)).astype(BF16)

    for i, d in enumerate((3, 5)):
        wait_for(za1.at[i], r_za.at[i, 0])
        add3(pa.at[0, at_z(d), pl.ds(2 * i, 2)], za1.at[i])
        send(pa.at[0, at_z(d)], za2.at[i, 0], s_za.at[i, 1], r_za.at[i, 1], z_next[i])

    settle("b", 0)
    for i in range(2):
        wait_for(zb2.at[i, 2], r_zb.at[i, 3])
    add(pb.at[0], rb.at[0], zb2.at[0, 2], zb2.at[1, 2])
    for i in range(2):
        send(pb.at[0, at_x(2), pl.ds(2 * i, 2)], xb1.at[i], s_xb.at[i, 0], r_xb.at[i, 0], x_next[i])

    for i, d in enumerate((2, 6)):
        wait_for(za2.at[i, 0], r_za.at[i, 1])
        add3(pa.at[0, at_z(d)], za2.at[i, 0])
        send(pa.at[0, at_z(d)], za2.at[i, 1], s_za.at[i, 2], r_za.at[i, 2], z_next[i])
    for i, d in enumerate((1, 3)):
        wait_for(xb1.at[i], r_xb.at[i, 0])
        add3(pb.at[0, at_x(d), pl.ds(2 * i, 2)], xb1.at[i])
        send(pb.at[0, at_x(d)], xb2.at[i], s_xb.at[i, 1], r_xb.at[i, 1], x_next[i])
    for i, d in enumerate((1, 7)):
        wait_for(za2.at[i, 1], r_za.at[i, 2])
        add3(pa.at[0, at_z(d)], za2.at[i, 1])
        send(pa.at[0, at_z(d)], za2.at[i, 2], s_za.at[i, 3], r_za.at[i, 3], z_next[i])

    for i in range(2):
        wait_for(xb2.at[i], r_xb.at[i, 1])
    for b in range(4):
        out[:, (4 + b) * B : (5 + b) * B] = (
            pb[0, x, b].astype(F32) + xb2[0, b].astype(F32) + xb2[1, b].astype(F32)
        )
    for i in range(2):
        wait_for(za2.at[i, 2], r_za.at[i, 3])
    for b in range(4):
        out[:, b * B : (b + 1) * B] = (
            pa[0, z, b].astype(F32) + za2[0, 2, b].astype(F32) + za2[1, 2, b].astype(F32)
        )
    for cp in pending:
        cp.wait_send()


def gather(part):
    any_spec = pl.BlockSpec(memory_space=pl.ANY)
    vmem = pl.BlockSpec(memory_space=pltpu.VMEM)
    dma = pltpu.SemaphoreType.DMA
    return pl.pallas_call(
        gather_kernel,
        out_shape=jax.ShapeDtypeStruct((LM, FLUX_DEV * B), F32),
        in_specs=[any_spec],
        out_specs=vmem,
        scratch_shapes=[
            pltpu.VMEM((NX, NZ, 4, LM, B), BF16),
            pltpu.VMEM((NZ, NX, 4, LM, B), BF16),
            pltpu.VMEM((NX, NZ, 4, LM, B), BF16),
            pltpu.VMEM((NZ, NX, 4, LM, B), BF16),
            pltpu.VMEM((2, 4, 4, LM, B), BF16),
            pltpu.VMEM((2, NZ, 4, LM, B), BF16),
            pltpu.VMEM((2, 2, 4, LM, B), BF16),
            pltpu.VMEM((2, 3, NX, 4, LM, B), BF16),
            pltpu.VMEM((2, 2, LM, B), BF16),
            pltpu.VMEM((2, 3, 4, LM, B), BF16),
            pltpu.VMEM((2, 2, LM, B), BF16),
            pltpu.VMEM((2, 4, LM, B), BF16),
            dma((NX,)), dma((NZ,)), dma((NX,)), dma((NX,)), dma((NZ,)), dma((NZ,)),
            dma((2, 2)), dma((2, 2)), dma((2, 4)), dma((2, 4)),
            dma((2, 4)), dma((2, 4)), dma((2, 2)), dma((2, 2)),
        ],
        compiler_params=pltpu.CompilerParams(
            collective_id=1, has_side_effects=True, vmem_limit_bytes=40 * 2**20
        ),
        name="gather",
    )(part.reshape(NZ, NX, 2, FLUX_DEV, LM, B))


def body(footprints, tile_row, tile_col, prior_flux, observed, precision_weight):
    source, coded = route(tile_row, tile_col)
    tiles, anoms, codes = spread(source, coded, footprints, prior_flux)
    weight = precision_weight.reshape(SOUND_DEV, 1, B)
    part = local(codes, tiles, anoms, observed, weight)
    return gather(part)


def solution(mesh):
    in_specs = (
        P("tile", None, None),
        P("tile"),
        P("tile"),
        P("mem", "tile"),
        P("mem", "tile"),
        P("tile"),
    )
    out_specs = P("mem", "tile")
    return jax.shard_map(body, mesh=mesh, in_specs=in_specs, out_specs=out_specs, check_vma=False)
```

time: 409 us -> 165 us (0.40)
  waiting for transfers between devices: 283 us -> 0 us
  Pallas kernels: 0 us -> 149 us
  starting transfers between devices: 39.3 us -> 0 us
  local copies, waits for them, and re-layouts: 31.6 us -> 14.9 us
  other arithmetic: 17.4 us -> 1.02 us
  matrix products: 14.4 us -> 0 us
  between operations: 13.6 us -> 0.09 us
  blocking collectives: 8.61 us -> 0 us
    all_to_all x5 -> x0, waiting for transfers between devices: 215 us -> none  [the longest x1 73.1 us: body(): lax.all_to_all(sent_back.astype(jnp.bfloat16), 'tile', split_axis=1, conc...]
    pallas_call x0 -> x3, Pallas kernels: none -> 149 us  [the longest x1 79.3 us: spread(): pl.pallas_call(spread_kernel, out_shape=(jax.ShapeDtypeStruct((NY, NT, CA...]
    all_gather x1 -> x0, waiting for transfers between devices: 68.2 us -> none  [body(): gathered = lax.all_gather(member_deviations, 'tile', axis=1, tiled=True)]
    all_to_all x5 -> x0, starting transfers between devices: 39.3 us -> none  [the longest x1 11.9 us: body(): lax.all_to_all(row_index[None, :], 'tile', split_axis=1, concat_axis=1, t...]
    gather x7 -> x0, local copies, waits for them, and re-layouts: 17.4 us -> none  [the longest x1 5.55 us: body(): jnp.take(gathered.reshape(local_members, -1, tile_size), tile_col, axis=1)]
    dot_general x4 -> x0, matrix products: 14.4 us -> none  [the longest x1 5.75 us: body(): jnp.einsum('mtk,trk->mtr', retrieved_blocks, footprints, preferred_elemen...]
    unnamed x4 -> x15, local copies, waits for them, and re-layouts: 2.68 us -> 14.8 us
    convert_element_type x3 -> x0, other arithmetic: 10.1 us -> none  [the longest x1 4.26 us: body(): sent_terms.astype(jnp.bfloat16)]
  transfers between devices with their start and end apart: 6 -> 0, of which waited for: 4 -> 0; matrix products, arithmetic and copies ran while one was open for 12% -> 0% of each run, Pallas kernels for 0% -> 0%
where the time goes in v1:
time: 165 us
  Pallas kernels  149 us (90%)
  local copies, waits for them, and re-layouts  14.9 us (9%)
    pallas_call x1, Pallas kernels, spread(): pl.pallas_call(spread_kernel, out_shape=(jax.ShapeDtypeStruct((NY, NT, CA...  79.3 us
    pallas_call x1, Pallas kernels, gather(): pl.pallas_call(gather_kernel, out_shape=jax.ShapeDtypeStruct((LM, FLUX_DE...  45.5 us
    pallas_call x1, Pallas kernels, local(): pl.pallas_call(local_kernel, out_shape=jax.ShapeDtypeStruct((NT * FLUX_DE...  23.7 us
    unnamed x15, local copies, waits for them, and re-layouts  14.8 us

profile of v1, /device:TPU:8, one launch (start us, length us, event | category | flops | bytes accessed | tf_op | source)
XLA Modules:
  0.0 164.6 jit_solution(14408036907602753482)
XLA Ops:
  0.0 0.7 and_select_fusion.1
  0.7 0.2 convert_reduce_fusion
  0.9 0.2 select_reduce_fusion
  1.0 0.1 select_n.32
  1.2 0.0 copy-start.3
  1.2 2.2 %copy-done.3 = bf16[128,128,128]{2,1,0:T(8,128)(2,1)S(1)} copy-done((bf16[128,128,128]{2,1,0:T(8,128)(2,1)S(1)}, bf16[128,128,128]{2,1,0:T(8,128)(2,1)}, u32[]{:S(2)}) %copy-start.3) | copy-done | bytes 4194328
  3.4 0.0 copy-start.5
  3.4 0.9 copy-done.5
  4.3 79.3 %spread.1 = (bf16[4,64,3,32,128]{4,3,2,1,0:T(8,128)(2,1)S(1)}, bf16[64,8,64,128]{3,2,1,0:T(8,128)(2,1)S(1)}, s32[64,1,128]{2,1,0:T(1,128)S(1)}) custom-call(s32[192]{0:T(256)S(1)} %get-tuple-element.12.source, s32[64,1,128]{2,1,0:T(1,128)S(1)} %bitcast.6, bf16[128,128,128]{2,1,0:T(8,128)(2,1)S(1)} %copy-done.3, bf16[64,1024]{1,0:T(8,128)(2,1)S(1)} %copy-done.5), custom_call_target="tpu_custom_call" | custom-call | tf_op jit(solution)/shard_map/spread/pallas_call | solution.py:277
  83.6 0.0 copy-start.1
  83.6 3.2 %copy-done.1 = bf16[64,8,64,128]{3,2,1,0:T(8,128)(2,1)} copy-done((bf16[64,8,64,128]{3,2,1,0:T(8,128)(2,1)}, bf16[64,8,64,128]{3,2,1,0:T(8,128)(2,1)S(1)}, u32[]{:S(2)}) %copy-start.1) | copy-done | bytes 8388632
  86.8 0.0 copy-start.2
  86.8 2.6 %copy-done.2 = bf16[4,64,3,32,128]{4,3,2,1,0:T(8,128)(2,1)} copy-done((bf16[4,64,3,32,128]{4,3,2,1,0:T(8,128)(2,1)}, bf16[4,64,3,32,128]{4,3,2,1,0:T(8,128)(2,1)S(1)}, u32[]{:S(2)}) %copy-start.2) | copy-done | bytes 6291480
  89.5 0.0 copy-start.4
  89.5 1.0 copy-done.4
  90.5 0.0 copy-start.6
  90.5 0.7 copy-done.6
  91.2 23.7 %local.1 = bf16[512,64,128]{2,1,0:T(8,128)(2,1)} custom-call(s32[64,1,128]{2,1,0:T(1,128)S(1)} %get-tuple-element.8.codes, bf16[4,64,3,32,128]{4,3,2,1,0:T(8,128)(2,1)} %copy-done.2, bf16[512,64,128]{2,1,0:T(8,128)(2,1)} %bitcast.5, f32[64,2048]{1,0:T(8,128)S(1)} %copy-done.4, s32[16,1,128]{2,1,0:T(1,128)S(1)} %bitcast.7), custom_call_target="tpu_custom_call" | custom-call | tf_op jit(solution)/shard_map/local/pallas_call | solution.py:375
  114.9 0.0 copy-start
  114.9 3.4 %copy-done = bf16[512,64,128]{2,1,0:T(8,128)(2,1)S(1)} copy-done((bf16[512,64,128]{2,1,0:T(8,128)(2,1)S(1)}, bf16[512,64,128]{2,1,0:T(8,128)(2,1)}, u32[]{:S(2)}) %copy-start) | copy-done | bytes 8388632
  118.3 45.5 %gather.1 = f32[64,1024]{1,0:T(8,128)S(1)} custom-call(bf16[8,4,2,8,64,128]{5,4,3,2,1,0:T(8,128)(2,1)S(1)} %bitcast.4), custom_call_target="tpu_custom_call" | custom-call | tf_op jit(solution)/shard_map/gather/pallas_call | solution.py:558
  163.9 0.7 copy.8
  (3 shorter events, 0.0 us)
Async XLA Ops:
  1.2 2.2 %copy-start.3 = (bf16[128,128,128]{2,1,0:T(8,128)(2,1)S(1)}, bf16[128,128,128]{2,1,0:T(8,128)(2,1)}, u32[]{:S(2)}) copy-start(bf16[128,128,128]{2,1,0:T(8,128)(2,1)} %footprints.1) | copy-start | bytes 12582916
  3.4 0.9 copy-start.5
  83.6 3.2 %copy-start.1 = (bf16[64,8,64,128]{3,2,1,0:T(8,128)(2,1)}, bf16[64,8,64,128]{3,2,1,0:T(8,128)(2,1)S(1)}, u32[]{:S(2)}) copy-start(bf16[64,8,64,128]{3,2,1,0:T(8,128)(2,1)S(1)} %get-tuple-element.10) | copy-start | bytes 25165828
  86.8 2.6 %copy-start.2 = (bf16[4,64,3,32,128]{4,3,2,1,0:T(8,128)(2,1)}, bf16[4,64,3,32,128]{4,3,2,1,0:T(8,128)(2,1)S(1)}, u32[]{:S(2)}) copy-start(bf16[4,64,3,32,128]{4,3,2,1,0:T(8,128)(2,1)S(1)} %get-tuple-element.9.tiles_h) | copy-start | bytes 18874372
  89.5 1.0 copy-start.4
  90.5 0.7 copy-start.6
  114.9 3.4 %copy-start = (bf16[512,64,128]{2,1,0:T(8,128)(2,1)S(1)}, bf16[512,64,128]{2,1,0:T(8,128)(2,1)}, u32[]{:S(2)}) copy-start(bf16[512,64,128]{2,1,0:T(8,128)(2,1)} %local.1) | copy-start | bytes 25165828

commit v2 on v1

--- a/solution.py
+++ b/solution.py
@@ -34,9 +34,9 @@
 
 
 def spread_kernel(
-    source, coded, footprints, prior, tiles, anoms, codes,
-    quarter, staged, sums, shard,
-    s_fp, s_sum, r_sum, s_tile, r_tile, s_code, r_code, s_y, r_y, r_y2,
+    source, coded, footprints, prior_h, tiles, anoms, codes,
+    prior, quarter, staged, sums, shard,
+    s_fp, s_prior, s_sum, r_sum, s_tile, r_tile, s_code, r_code, s_y, r_y, r_y2,
     s_local, s_z, r_z, s_x, r_x, r_x2, s_sib, r_sib,
 ):
     me = lax.axis_index("tile")
@@ -67,6 +67,8 @@
     def wait_for(ref, sem):
         pltpu.make_async_copy(ref, ref, sem).wait()
 
+    prior_copy = pltpu.make_async_copy(prior_h, prior, s_prior)
+    prior_copy.start()
     fp_copy = pltpu.make_async_copy(
         footprints.at[:, pl.ds(pl.multiple_of(q * 32, 32), 32), :], quarter, s_fp
     )
@@ -85,6 +87,7 @@
             barrier, inc=1, device_id={"tile": me, "mem": at_y(o)}, device_id_type=MESH
         )
 
+    prior_copy.wait()
     for j in range(FLUX_DEV):
         part = jnp.sum(prior[:, j * B : (j + 1) * B].astype(F32), axis=0, keepdims=True)
         sums[0, j : j + 1, :] = part
@@ -271,7 +274,7 @@
 
 
 def spread(source, coded, footprints, prior):
-    any_spec = pl.BlockSpec(memory_space=pl.ANY)
+    hbm = pl.BlockSpec(memory_space=pltpu.HBM)
     vmem = pl.BlockSpec(memory_space=pltpu.VMEM)
     dma = pltpu.SemaphoreType.DMA
     return pl.pallas_call(
@@ -281,14 +284,15 @@
             jax.ShapeDtypeStruct((NT, FLUX_DEV, LM, B), BF16),
             jax.ShapeDtypeStruct((NT, 1, B), jnp.int32),
         ),
-        in_specs=[pl.BlockSpec(memory_space=pltpu.SMEM), vmem, any_spec, vmem],
-        out_specs=(any_spec, any_spec, any_spec),
+        in_specs=[pl.BlockSpec(memory_space=pltpu.SMEM), vmem, hbm, hbm],
+        out_specs=(vmem, vmem, vmem),
         scratch_shapes=[
+            pltpu.VMEM((LM, FLUX_DEV * B), BF16),
             pltpu.VMEM((B, 32, B), BF16),
             pltpu.VMEM((NT, CAP, 32, B), BF16),
             pltpu.VMEM((NY, FLUX_DEV, B), F32),
             pltpu.VMEM((FLUX_DEV, LM, B), BF16),
-            dma, dma((NY,)), dma((NY,)), dma, dma((NZ,)), dma, dma,
+            dma, dma, dma((NY,)), dma((NY,)), dma, dma((NZ,)), dma, dma,
             dma((4, NZ)), dma((2, NZ)), dma((2, NZ)),
             dma, dma((2, 5)), dma((2, 5)), dma((4, NZ)), dma((2, NZ)), dma((2, NZ)),
             dma((NX, NZ)), dma((NX, NZ)),
@@ -301,21 +305,14 @@
 
 
 def local_kernel(
-    codes, tiles_h, anoms_h, observed, weight, out_h,
-    tiles, anoms, modelled, weighted, total, packed, s_tiles, s_anoms, s_out,
+    codes, tiles, anoms, observed_h, weight_h, out,
+    observed, weight, modelled, weighted, total, s_obs, s_weight,
 ):
-    anoms_in = pltpu.make_async_copy(anoms_h, anoms, s_anoms)
-    anoms_in.start()
-    tiles_in = pltpu.make_async_copy(tiles_h, tiles, s_tiles)
-    tiles_in.start()
+    observed_in = pltpu.make_async_copy(observed_h, observed, s_obs)
+    observed_in.start()
+    weight_in = pltpu.make_async_copy(weight_h, weight, s_weight)
+    weight_in.start()
     modelled[...] = jnp.zeros_like(modelled)
-
-    @pl.loop(0, 64)
-    def _(i):
-        total[pl.ds(i * 8, 8)] = jnp.zeros((8, LM, B), F32)
-
-    anoms_in.wait()
-    tiles_in.wait()
     step = 2
 
     def fetch(i, o, s):
@@ -333,9 +330,12 @@
                     anoms[col], tile, (((1,), (1,)), ((), ())), preferred_element_type=F32
                 )
                 terms.append((row, term))
+        total[pl.ds(i * 16, 16)] = jnp.zeros((16, LM, B), F32)
         for row, term in terms:
             modelled[row] += term
 
+    observed_in.wait()
+    weight_in.wait()
     for r in range(SOUND_DEV):
         factor = weight[r].astype(F32) / 8.0
         gap = modelled[r] - observed[:, r * B : (r + 1) * B]
@@ -355,38 +355,29 @@
         for col, term in terms:
             total[col] += term
 
-    @pl.loop(0, 8)
+    @pl.loop(0, NT)
     def _(i):
-        @pl.loop(0, 8)
-        def _(j):
-            packed[pl.ds((i * 8 + j) * 8, 8)] = total[pl.ds((i * 8 + j) * 8, 8)].astype(BF16)
-
-        pltpu.make_async_copy(
-            packed.at[pl.ds(i * 64, 64)], out_h.at[pl.ds(i * 64, 64)], s_out
-        ).start()
-
-    pltpu.make_async_copy(packed, out_h, s_out).wait()
+        out[pl.ds(i * 8, 8)] = total[pl.ds(i * 8, 8)].astype(BF16)
 
 
 def local(codes, tiles, anoms, observed, weight):
-    any_spec = pl.BlockSpec(memory_space=pl.ANY)
+    hbm = pl.BlockSpec(memory_space=pltpu.HBM)
     vmem = pl.BlockSpec(memory_space=pltpu.VMEM)
     dma = pltpu.SemaphoreType.DMA
     return pl.pallas_call(
         local_kernel,
         out_shape=jax.ShapeDtypeStruct((NT * FLUX_DEV, LM, B), BF16),
-        in_specs=[pl.BlockSpec(memory_space=pltpu.SMEM), any_spec, any_spec, vmem, vmem],
-        out_specs=any_spec,
+        in_specs=[pl.BlockSpec(memory_space=pltpu.SMEM), vmem, vmem, hbm, hbm],
+        out_specs=vmem,
         scratch_shapes=[
-            pltpu.VMEM((NY, NT, CAP, 32, B), BF16),
-            pltpu.VMEM((NT * FLUX_DEV, LM, B), BF16),
+            pltpu.VMEM((LM, SOUND_DEV * B), F32),
+            pltpu.VMEM((SOUND_DEV, 1, B), jnp.int32),
             pltpu.VMEM((SOUND_DEV + 1, LM, B), F32),
             pltpu.VMEM((SOUND_DEV + 1, LM, B), BF16),
             pltpu.VMEM((NT * FLUX_DEV, LM, B), F32),
-            pltpu.VMEM((NT * FLUX_DEV, LM, B), BF16),
-            dma, dma, dma,
+            dma, dma,
         ],
-        compiler_params=pltpu.CompilerParams(vmem_limit_bytes=50 * 2**20),
+        compiler_params=pltpu.CompilerParams(vmem_limit_bytes=22 * 2**20),
         name="local",
     )(codes, tiles, anoms.reshape(NT * FLUX_DEV, LM, B), observed, weight)
 
@@ -394,7 +385,7 @@
 def gather_kernel(
     part, out,
     pa, pb, ra, rb, xa1, xa2, zb1, zb2, za1, za2, xb1, xb2,
-    s_own_a, s_own_b, s_sib_a, r_sib_a, s_sib_b, r_sib_b,
+    s_sib_a, r_sib_a, s_sib_b, r_sib_b,
     s_xa, r_xa, s_zb, r_zb, s_za, r_za, s_xb, r_xb,
 ):
     me = lax.axis_index("tile")
@@ -429,16 +420,8 @@
     def wait_for(ref, sem):
         pltpu.make_async_copy(ref, ref, sem).wait()
 
-    def own(kind, d):
-        if kind == "a":
-            return part.at[:, at_x(d), core, pl.ds(0, 4)], pa.at[d], s_own_a.at[d]
-        return part.at[at_z(d), :, core, pl.ds(4, 4)], pb.at[d], s_own_b.at[d]
-
     order = [("a", 2), ("b", 4), ("b", 3), ("b", 5), ("a", 1), ("a", 3),
              ("b", 2), ("b", 6), ("b", 1), ("b", 7), ("b", 0), ("a", 0)]
-    for kind, d in order:
-        pltpu.make_async_copy(*own(kind, d)).start()
-
     barrier = pltpu.get_barrier_semaphore()
     for t in (sibling, *x_next, *z_next):
         pl.semaphore_signal(barrier, inc=1, device_id={"tile": t, "mem": q}, device_id_type=MESH)
@@ -450,28 +433,33 @@
         else:
             send(part.at[at_z(d), :, 1 - core, pl.ds(4, 4)], rb.at[d], s_sib_b.at[d], r_sib_b.at[d], sibling)
 
-    def add(dst, *srcs):
+    def total(first, *rest):
+        value = first.astype(F32)
+        for r in rest:
+            value = value + r.astype(F32)
+        return value.astype(BF16)
+
+    def add(dst, src):
         @pl.loop(0, dst.shape[0])
         def _(i):
             for b in range(dst.shape[1]):
-                value = dst[i, b].astype(F32)
-                for s in srcs:
-                    value = value + s[i, b].astype(F32)
-                dst[i, b] = value.astype(BF16)
-
-    def settle(kind, d):
-        pltpu.make_async_copy(*own(kind, d)).wait()
+                dst[i, b] = total(dst[i, b], src[i, b])
+
+    def pair(kind, d, *more):
         if kind == "a":
             wait_for(ra.at[d], r_sib_a.at[d])
+
+            @pl.loop(0, NZ)
+            def _(i):
+                for b in range(4):
+                    pa[d, i, b] = total(part[i, at_x(d), core, b], ra[d, i, b], *(m[i, b] for m in more))
         else:
             wait_for(rb.at[d], r_sib_b.at[d])
 
-    def pair(kind, d):
-        settle(kind, d)
-        if kind == "a":
-            add(pa.at[d], ra.at[d])
-        else:
-            add(pb.at[d], rb.at[d])
+            @pl.loop(0, NX)
+            def _(i):
+                for b in range(4):
+                    pb[d, i, b] = total(part[at_z(d), i, core, 4 + b], rb[d, i, b], *(m[i, b] for m in more))
 
     pair("a", 2)
     for i in range(2):
@@ -499,10 +487,9 @@
             add(pb.at[d], zb2.at[i, step - 1])
             send(pb.at[d], zb2.at[i, step], s_zb.at[i, step + 1], r_zb.at[i, step + 1], z_next[i])
 
-    settle("a", 0)
     for i in range(2):
         wait_for(xa2.at[i], r_xa.at[i, 1])
-    add(pa.at[0], ra.at[0], xa2.at[0], xa2.at[1])
+    pair("a", 0, xa2.at[0], xa2.at[1])
     for i in range(2):
         send(pa.at[0, at_z(4), pl.ds(2 * i, 2)], za1.at[i], s_za.at[i, 0], r_za.at[i, 0], z_next[i])
 
@@ -515,10 +502,9 @@
         add3(pa.at[0, at_z(d), pl.ds(2 * i, 2)], za1.at[i])
         send(pa.at[0, at_z(d)], za2.at[i, 0], s_za.at[i, 1], r_za.at[i, 1], z_next[i])
 
-    settle("b", 0)
     for i in range(2):
         wait_for(zb2.at[i, 2], r_zb.at[i, 3])
-    add(pb.at[0], rb.at[0], zb2.at[0, 2], zb2.at[1, 2])
+    pair("b", 0, zb2.at[0, 2], zb2.at[1, 2])
     for i in range(2):
         send(pb.at[0, at_x(2), pl.ds(2 * i, 2)], xb1.at[i], s_xb.at[i, 0], r_xb.at[i, 0], x_next[i])
 
@@ -552,13 +538,12 @@
 
 
 def gather(part):
-    any_spec = pl.BlockSpec(memory_space=pl.ANY)
     vmem = pl.BlockSpec(memory_space=pltpu.VMEM)
     dma = pltpu.SemaphoreType.DMA
     return pl.pallas_call(
         gather_kernel,
         out_shape=jax.ShapeDtypeStruct((LM, FLUX_DEV * B), F32),
-        in_specs=[any_spec],
+        in_specs=[vmem],
         out_specs=vmem,
         scratch_shapes=[
             pltpu.VMEM((NX, NZ, 4, LM, B), BF16),
@@ -573,21 +558,23 @@
             pltpu.VMEM((2, 3, 4, LM, B), BF16),
             pltpu.VMEM((2, 2, LM, B), BF16),
             pltpu.VMEM((2, 4, LM, B), BF16),
-            dma((NX,)), dma((NZ,)), dma((NX,)), dma((NX,)), dma((NZ,)), dma((NZ,)),
+            dma((NX,)), dma((NX,)), dma((NZ,)), dma((NZ,)),
             dma((2, 2)), dma((2, 2)), dma((2, 4)), dma((2, 4)),
             dma((2, 4)), dma((2, 4)), dma((2, 2)), dma((2, 2)),
         ],
         compiler_params=pltpu.CompilerParams(
-            collective_id=1, has_side_effects=True, vmem_limit_bytes=40 * 2**20
+            collective_id=1, has_side_effects=True, vmem_limit_bytes=18 * 2**20
         ),
         name="gather",
     )(part.reshape(NZ, NX, 2, FLUX_DEV, LM, B))
 
 
 def body(footprints, tile_row, tile_col, prior_flux, observed, precision_weight):
+    pin = functools.partial(pltpu.with_memory_space_constraint, memory_space=pltpu.HBM)
+    footprints, prior_flux, observed = pin(footprints), pin(prior_flux), pin(observed)
     source, coded = route(tile_row, tile_col)
     tiles, anoms, codes = spread(source, coded, footprints, prior_flux)
-    weight = precision_weight.reshape(SOUND_DEV, 1, B)
+    weight = pin(precision_weight.reshape(SOUND_DEV, 1, B))
     part = local(codes, tiles, anoms, observed, weight)
     return gather(part)
 

time: 165 us -> 143 us (0.87)
  local copies, waits for them, and re-layouts: 14.9 us -> 0.84 us
  Pallas kernels: 149 us -> 141 us
    unnamed x15 -> x1, local copies, waits for them, and re-layouts: 14.8 us -> 0.71 us
    pallas_call x1, Pallas kernels: 23.7 us -> 16.3 us  [local(): pl.pallas_call(local_kernel, out_shape=jax.ShapeDtypeStruct((NT * FLUX_DE...]
where the time goes in v2:
time: 143 us
  Pallas kernels  141 us (99%)
    pallas_call x1, Pallas kernels, spread(): pl.pallas_call(spread_kernel, out_shape=(jax.ShapeDtypeStruct((NY, NT, CA...  79.4 us
    pallas_call x1, Pallas kernels, gather(): pl.pallas_call(gather_kernel, out_shape=jax.ShapeDtypeStruct((LM, FLUX_DE...  45.2 us
    pallas_call x1, Pallas kernels, local(): pl.pallas_call(local_kernel, out_shape=jax.ShapeDtypeStruct((NT * FLUX_DE...  16.3 us

profile of v2, /device:TPU:8, one launch (start us, length us, event | category | flops | bytes accessed | tf_op | source)
XLA Modules:
  0.0 142.8 jit_solution(490691372083948209)
XLA Ops:
  0.0 0.7 and_select_fusion.1
  0.7 0.2 convert_reduce_fusion
  0.9 0.2 select_reduce_fusion
  1.0 0.1 select_n.32
  1.2 79.4 %spread.1 = (bf16[4,64,3,32,128]{4,3,2,1,0:T(8,128)(2,1)S(1)}, bf16[64,8,64,128]{3,2,1,0:T(8,128)(2,1)S(1)}, s32[64,1,128]{2,1,0:T(1,128)S(1)}) custom-call(s32[192]{0:T(256)S(1)} %get-tuple-element.12.source, s32[64,1,128]{2,1,0:T(1,128)S(1)} %bitcast.6, bf16[128,128,128]{2,1,0:T(8,128)(2,1)} %footprints.1, bf16[64,1024]{1,0:T(8,128)(2,1)} %prior_h.1), custom_call_target="tpu_custom_call" | custom-call | tf_op jit(solution)/shard_map/spread/pallas_call | solution.py:280
  80.5 16.3 %local.1 = bf16[512,64,128]{2,1,0:T(8,128)(2,1)S(1)} custom-call(s32[64,1,128]{2,1,0:T(1,128)S(1)} %get-tuple-element.8.codes, bf16[4,64,3,32,128]{4,3,2,1,0:T(8,128)(2,1)S(1)} %get-tuple-element.9.tiles, bf16[512,64,128]{2,1,0:T(8,128)(2,1)S(1)} %bitcast.5, f32[64,2048]{1,0:T(8,128)} %observed_h.1, s32[16,1,128]{2,1,0:T(1,128)} %bitcast.7), custom_call_target="tpu_custom_call" | custom-call | tf_op jit(solution)/shard_map/local/pallas_call | solution.py:367
  96.8 45.2 %gather.1 = f32[64,1024]{1,0:T(8,128)S(1)} custom-call(bf16[8,4,2,8,64,128]{5,4,3,2,1,0:T(8,128)(2,1)S(1)} %bitcast.4), custom_call_target="tpu_custom_call" | custom-call | tf_op jit(solution)/shard_map/gather/pallas_call | solution.py:543
  142.1 0.7 copy.8
  (3 shorter events, 0.0 us)

commit v3 on v2

--- a/solution.py
+++ b/solution.py
@@ -382,11 +382,19 @@
     )(codes, tiles, anoms.reshape(NT * FLUX_DEV, LM, B), observed, weight)
 
 
+NA = 5
+NB = FLUX_DEV - NA
+FAR_X = ((4, 3, 2, 1), (5, 6, 7, 0))
+NEAR_X = (4, 5, 3, 6, 2, 7, 1, 0)
+FAR_Z = ((2, 1), (3, 0))
+NEAR_Z = (2, 1, 3, 0)
+
+
 def gather_kernel(
     part, out,
     pa, pb, ra, rb, xa1, xa2, zb1, zb2, za1, za2, xb1, xb2,
     s_sib_a, r_sib_a, s_sib_b, r_sib_b,
-    s_xa, r_xa, s_zb, r_zb, s_za, r_za, s_xb, r_xb,
+    s_xa1, r_xa1, s_xa2, r_xa2, s_zb1, r_zb1, s_zb2, r_zb2, s_za, r_za, s_xb, r_xb,
 ):
     me = lax.axis_index("tile")
     q = lax.axis_index("mem")
@@ -420,119 +428,163 @@
     def wait_for(ref, sem):
         pltpu.make_async_copy(ref, ref, sem).wait()
 
-    order = [("a", 2), ("b", 4), ("b", 3), ("b", 5), ("a", 1), ("a", 3),
-             ("b", 2), ("b", 6), ("b", 1), ("b", 7), ("b", 0), ("a", 0)]
     barrier = pltpu.get_barrier_semaphore()
     for t in (sibling, *x_next, *z_next):
         pl.semaphore_signal(barrier, inc=1, device_id={"tile": t, "mem": q}, device_id_type=MESH)
     pl.semaphore_wait(barrier, 5)
 
-    for kind, d in order:
+    for kind, d in (("b", 4), ("a", 2), ("b", 3), ("b", 5), ("a", 1), ("a", 3),
+                    ("b", 2), ("b", 6), ("b", 1), ("b", 7), ("a", 0), ("b", 0)):
         if kind == "a":
-            send(part.at[:, at_x(d), 1 - core, pl.ds(0, 4)], ra.at[d], s_sib_a.at[d], r_sib_a.at[d], sibling)
+            send(part.at[:, at_x(d), 1 - core, pl.ds(0, NA)], ra.at[d], s_sib_a.at[d], r_sib_a.at[d], sibling)
         else:
-            send(part.at[at_z(d), :, 1 - core, pl.ds(4, 4)], rb.at[d], s_sib_b.at[d], r_sib_b.at[d], sibling)
-
-    def total(first, *rest):
-        value = first.astype(F32)
-        for r in rest:
-            value = value + r.astype(F32)
-        return value.astype(BF16)
-
-    def add(dst, src):
-        @pl.loop(0, dst.shape[0])
-        def _(i):
-            for b in range(dst.shape[1]):
-                dst[i, b] = total(dst[i, b], src[i, b])
-
-    def pair(kind, d, *more):
-        if kind == "a":
+            send(part.at[at_z(d), :, 1 - core, pl.ds(NA, NB)], rb.at[d], s_sib_b.at[d], r_sib_b.at[d], sibling)
+
+    settled = set()
+
+    def from_a(d, zz):
+        if ("a", d) not in settled:
+            settled.add(("a", d))
             wait_for(ra.at[d], r_sib_a.at[d])
-
-            @pl.loop(0, NZ)
-            def _(i):
-                for b in range(4):
-                    pa[d, i, b] = total(part[i, at_x(d), core, b], ra[d, i, b], *(m[i, b] for m in more))
+        return [part.at[zz, at_x(d), core], ra.at[d, zz]]
+
+    def from_b(d, xx):
+        if ("b", d) not in settled:
+            settled.add(("b", d))
+            wait_for(rb.at[d], r_sib_b.at[d])
+        return [part.at[at_z(d), xx, core, pl.ds(NA, NB)], rb.at[d, xx]]
+
+    def total(dst, sources, first, last):
+        @pl.loop(first, last)
+        def _(b):
+            value = None
+            for s in sources:
+                ref, start = s if isinstance(s, tuple) else (s, 0)
+                v = ref[b - start].astype(F32)
+                value = v if value is None else value + v
+            dst[b] = value.astype(BF16)
+
+    def result(base, sources, count):
+        for b in range(count):
+            value = None
+            for s in sources:
+                v = s[b].astype(F32)
+                value = v if value is None else value + v
+            out[:, (base + b) * B : (base + b + 1) * B] = value
+
+    def a_far(k):
+        for i in range(2):
+            zz = at_z(FAR_X[i][k])
+            total(pa.at[2, zz], from_a(2, zz), 0, NA)
+            send(pa.at[2, zz], xa1.at[i, k], s_xa1.at[i, k], r_xa1.at[i, k], x_next[i])
+
+    def a_near(j):
+        oz = NEAR_X[j]
+        zz = at_z(oz)
+        for i, d in enumerate((1, 3)):
+            sources = from_a(d, zz)
+            if oz in FAR_X[i]:
+                k = FAR_X[i].index(oz)
+                wait_for(xa1.at[i, k], r_xa1.at[i, k])
+                sources.append(xa1.at[i, k])
+            total(pa.at[d, zz], sources, 0, NA)
+            send(pa.at[d, zz], xa2.at[i, j], s_xa2.at[i, j], r_xa2.at[i, j], x_next[i])
+
+    half_a, half_b = (NA + 1) // 2, (NB + 1) // 2
+
+    def a_own(oz):
+        j = NEAR_X.index(oz)
+        zz = at_z(oz)
+        for i in range(2):
+            wait_for(xa2.at[i, j], r_xa2.at[i, j])
+        sources = [*from_a(0, zz), xa2.at[0, j], xa2.at[1, j]]
+        mine = pa.at[0, zz]
+        if oz == 4:
+            total(mine, sources, 0, NA)
+            for i, (first, size) in enumerate(((0, half_a), (half_a, NA - half_a))):
+                piece = za1.at[pl.ds(first, size)]
+                send(mine.at[pl.ds(first, size)], piece, s_za.at[i, 0], r_za.at[i, 0], z_next[i])
+        elif oz in (3, 5):
+            i = (3, 5).index(oz)
+            first, size = ((0, half_a), (half_a, NA - half_a))[i]
+            wait_for(za1.at[pl.ds(first, size)], r_za.at[i, 0])
+            total(mine, [*sources, za1], first, first + size)
+            total(mine, sources, *((half_a, NA), (0, half_a))[i])
+            send(mine, za2.at[i, 0], s_za.at[i, 1], r_za.at[i, 1], z_next[i])
+        elif oz != 0:
+            i = 0 if oz < 4 else 1
+            step = 4 - oz if i == 0 else oz - 4
+            wait_for(za2.at[i, step - 2], r_za.at[i, step - 1])
+            total(mine, [*sources, za2.at[i, step - 2]], 0, NA)
+            send(mine, za2.at[i, step - 1], s_za.at[i, step], r_za.at[i, step], z_next[i])
         else:
-            wait_for(rb.at[d], r_sib_b.at[d])
-
-            @pl.loop(0, NX)
-            def _(i):
-                for b in range(4):
-                    pb[d, i, b] = total(part[at_z(d), i, core, 4 + b], rb[d, i, b], *(m[i, b] for m in more))
-
-    pair("a", 2)
-    for i in range(2):
-        send(pa.at[2, pl.ds(4 * i, 4)], xa1.at[i], s_xa.at[i, 0], r_xa.at[i, 0], x_next[i])
-    pair("b", 4)
-    for i in range(2):
-        send(pb.at[4, pl.ds(2 * i, 2)], zb1.at[i], s_zb.at[i, 0], r_zb.at[i, 0], z_next[i])
-    pair("b", 3)
-    pair("b", 5)
-    for i, d in enumerate((3, 5)):
-        wait_for(zb1.at[i], r_zb.at[i, 0])
-        add(pb.at[d, pl.ds(2 * i, 2)], zb1.at[i])
-        send(pb.at[d], zb2.at[i, 0], s_zb.at[i, 1], r_zb.at[i, 1], z_next[i])
-    pair("a", 1)
-    pair("a", 3)
-    for i, d in enumerate((1, 3)):
-        wait_for(xa1.at[i], r_xa.at[i, 0])
-        add(pa.at[d, pl.ds(4 * i, 4)], xa1.at[i])
-        send(pa.at[d], xa2.at[i], s_xa.at[i, 1], r_xa.at[i, 1], x_next[i])
-    for step in (1, 2):
-        pair("b", 3 - step)
-        pair("b", 5 + step)
-        for i, d in enumerate((3 - step, 5 + step)):
-            wait_for(zb2.at[i, step - 1], r_zb.at[i, step])
-            add(pb.at[d], zb2.at[i, step - 1])
-            send(pb.at[d], zb2.at[i, step], s_zb.at[i, step + 1], r_zb.at[i, step + 1], z_next[i])
-
-    for i in range(2):
-        wait_for(xa2.at[i], r_xa.at[i, 1])
-    pair("a", 0, xa2.at[0], xa2.at[1])
-    for i in range(2):
-        send(pa.at[0, at_z(4), pl.ds(2 * i, 2)], za1.at[i], s_za.at[i, 0], r_za.at[i, 0], z_next[i])
-
-    def add3(dst, src):
-        for b in range(dst.shape[0]):
-            dst[b] = (dst[b].astype(F32) + src[b].astype(F32)).astype(BF16)
-
-    for i, d in enumerate((3, 5)):
-        wait_for(za1.at[i], r_za.at[i, 0])
-        add3(pa.at[0, at_z(d), pl.ds(2 * i, 2)], za1.at[i])
-        send(pa.at[0, at_z(d)], za2.at[i, 0], s_za.at[i, 1], r_za.at[i, 1], z_next[i])
-
-    for i in range(2):
-        wait_for(zb2.at[i, 2], r_zb.at[i, 3])
-    pair("b", 0, zb2.at[0, 2], zb2.at[1, 2])
-    for i in range(2):
-        send(pb.at[0, at_x(2), pl.ds(2 * i, 2)], xb1.at[i], s_xb.at[i, 0], r_xb.at[i, 0], x_next[i])
-
-    for i, d in enumerate((2, 6)):
-        wait_for(za2.at[i, 0], r_za.at[i, 1])
-        add3(pa.at[0, at_z(d)], za2.at[i, 0])
-        send(pa.at[0, at_z(d)], za2.at[i, 1], s_za.at[i, 2], r_za.at[i, 2], z_next[i])
-    for i, d in enumerate((1, 3)):
-        wait_for(xb1.at[i], r_xb.at[i, 0])
-        add3(pb.at[0, at_x(d), pl.ds(2 * i, 2)], xb1.at[i])
-        send(pb.at[0, at_x(d)], xb2.at[i], s_xb.at[i, 1], r_xb.at[i, 1], x_next[i])
-    for i, d in enumerate((1, 7)):
-        wait_for(za2.at[i, 1], r_za.at[i, 2])
-        add3(pa.at[0, at_z(d)], za2.at[i, 1])
-        send(pa.at[0, at_z(d)], za2.at[i, 2], s_za.at[i, 3], r_za.at[i, 3], z_next[i])
-
-    for i in range(2):
-        wait_for(xb2.at[i], r_xb.at[i, 1])
-    for b in range(4):
-        out[:, (4 + b) * B : (5 + b) * B] = (
-            pb[0, x, b].astype(F32) + xb2[0, b].astype(F32) + xb2[1, b].astype(F32)
-        )
-    for i in range(2):
-        wait_for(za2.at[i, 2], r_za.at[i, 3])
-    for b in range(4):
-        out[:, b * B : (b + 1) * B] = (
-            pa[0, z, b].astype(F32) + za2[0, 2, b].astype(F32) + za2[1, 2, b].astype(F32)
-        )
+            for i in range(2):
+                wait_for(za2.at[i, 2], r_za.at[i, 3])
+            result(0, [*sources, za2.at[0, 2], za2.at[1, 2]], NA)
+
+    def b_far(k):
+        for i in range(2):
+            xx = at_x(FAR_Z[i][k])
+            total(pb.at[4, xx], from_b(4, xx), 0, NB)
+            send(pb.at[4, xx], zb1.at[i, k], s_zb1.at[i, k], r_zb1.at[i, k], z_next[i])
+
+    def b_near(step, j):
+        ox = NEAR_Z[j]
+        xx = at_x(ox)
+        for i, d in enumerate((4 - step, 4 + step)):
+            sources = from_b(d, xx)
+            if step > 1:
+                wait_for(zb2.at[i, step - 2, j], r_zb2.at[i, step - 2, j])
+                sources.append(zb2.at[i, step - 2, j])
+            elif ox in FAR_Z[i]:
+                k = FAR_Z[i].index(ox)
+                wait_for(zb1.at[i, k], r_zb1.at[i, k])
+                sources.append(zb1.at[i, k])
+            total(pb.at[d, xx], sources, 0, NB)
+            send(
+                pb.at[d, xx], zb2.at[i, step - 1, j], s_zb2.at[i, step - 1, j], r_zb2.at[i, step - 1, j], z_next[i]
+            )
+
+    def b_own(ox):
+        j = NEAR_Z.index(ox)
+        xx = at_x(ox)
+        for i in range(2):
+            wait_for(zb2.at[i, 2, j], r_zb2.at[i, 2, j])
+        sources = [*from_b(0, xx), zb2.at[0, 2, j], zb2.at[1, 2, j]]
+        mine = pb.at[0, xx]
+        halves = ((0, half_b), (half_b, NB - half_b))
+        if ox == 2:
+            total(mine, sources, 0, NB)
+            for i, (first, size) in enumerate(halves):
+                piece = xb1.at[pl.ds(first, size)]
+                send(mine.at[pl.ds(first, size)], piece, s_xb.at[i, 0], r_xb.at[i, 0], x_next[i])
+        elif ox != 0:
+            i = (1, 3).index(ox)
+            first, size = halves[i]
+            wait_for(xb1.at[pl.ds(first, size)], r_xb.at[i, 0])
+            total(mine, [*sources, xb1], first, first + size)
+            total(mine, sources, *((half_b, NB), (0, half_b))[i])
+            send(mine, xb2.at[i], s_xb.at[i, 1], r_xb.at[i, 1], x_next[i])
+        else:
+            for i in range(2):
+                wait_for(xb2.at[i], r_xb.at[i, 1])
+            result(NA, [*sources, xb2.at[0], xb2.at[1]], NB)
+
+    events = []
+    for k in range(2):
+        events.append((1.9 + 0.3 * k, b_far, (k,)))
+    for k in range(4):
+        events.append((2.0 + 0.3 * k, a_far, (k,)))
+    for j in range(8):
+        events.append((4.0 + 1.7 * (j // 2 + 1), a_near, (j,)))
+        events.append((11.2 + 1.65 * (j + 1), a_own, (NEAR_X[j],)))
+    for j in range(4):
+        for step in (1, 2, 3):
+            events.append((4.0 * step + min(j + 1, 2 if step == 1 else 4), b_near, (step, j)))
+    for ox, when in ((2, 17.0), (1, 19.5), (3, 19.6), (0, 22.5)):
+        events.append((when, b_own, (ox,)))
+    for _, act, args in sorted(events, key=lambda e: e[0]):
+        act(*args)
     for cp in pending:
         cp.wait_send()
 
@@ -546,20 +598,21 @@
         in_specs=[vmem],
         out_specs=vmem,
         scratch_shapes=[
-            pltpu.VMEM((NX, NZ, 4, LM, B), BF16),
-            pltpu.VMEM((NZ, NX, 4, LM, B), BF16),
-            pltpu.VMEM((NX, NZ, 4, LM, B), BF16),
-            pltpu.VMEM((NZ, NX, 4, LM, B), BF16),
-            pltpu.VMEM((2, 4, 4, LM, B), BF16),
-            pltpu.VMEM((2, NZ, 4, LM, B), BF16),
-            pltpu.VMEM((2, 2, 4, LM, B), BF16),
-            pltpu.VMEM((2, 3, NX, 4, LM, B), BF16),
-            pltpu.VMEM((2, 2, LM, B), BF16),
-            pltpu.VMEM((2, 3, 4, LM, B), BF16),
-            pltpu.VMEM((2, 2, LM, B), BF16),
-            pltpu.VMEM((2, 4, LM, B), BF16),
+            pltpu.VMEM((NX, NZ, NA, LM, B), BF16),
+            pltpu.VMEM((NZ, NX, NB, LM, B), BF16),
+            pltpu.VMEM((NX, NZ, NA, LM, B), BF16),
+            pltpu.VMEM((NZ, NX, NB, LM, B), BF16),
+            pltpu.VMEM((2, 4, NA, LM, B), BF16),
+            pltpu.VMEM((2, NZ, NA, LM, B), BF16),
+            pltpu.VMEM((2, 2, NB, LM, B), BF16),
+            pltpu.VMEM((2, 3, NX, NB, LM, B), BF16),
+            pltpu.VMEM((NA, LM, B), BF16),
+            pltpu.VMEM((2, 3, NA, LM, B), BF16),
+            pltpu.VMEM((NB, LM, B), BF16),
+            pltpu.VMEM((2, NB, LM, B), BF16),
             dma((NX,)), dma((NX,)), dma((NZ,)), dma((NZ,)),
-            dma((2, 2)), dma((2, 2)), dma((2, 4)), dma((2, 4)),
+            dma((2, 4)), dma((2, 4)), dma((2, NZ)), dma((2, NZ)),
+            dma((2, 2)), dma((2, 2)), dma((2, 3, NX)), dma((2, 3, NX)),
             dma((2, 4)), dma((2, 4)), dma((2, 2)), dma((2, 2)),
         ],
         compiler_params=pltpu.CompilerParams(

time: 143 us -> 135 us (0.944)
  Pallas kernels: 141 us -> 133 us
    pallas_call x1, Pallas kernels: 45.2 us -> 37.1 us  [gather(): pl.pallas_call(gather_kernel, out_shape=jax.ShapeDtypeStruct((LM, FLUX_DE...]
where the time goes in v3:
time: 135 us
  Pallas kernels  133 us (99%)
    pallas_call x1, Pallas kernels, spread(): pl.pallas_call(spread_kernel, out_shape=(jax.ShapeDtypeStruct((NY, NT, CA...  79.4 us
    pallas_call x1, Pallas kernels, gather(): pl.pallas_call(gather_kernel, out_shape=jax.ShapeDtypeStruct((LM, FLUX_DE...  37.1 us
    pallas_call x1, Pallas kernels, local(): pl.pallas_call(local_kernel, out_shape=jax.ShapeDtypeStruct((NT * FLUX_DE...  16.3 us

profile of v3, /device:TPU:8, one launch (start us, length us, event | category | flops | bytes accessed | tf_op | source)
XLA Modules:
  0.0 134.7 jit_solution(7521743923045613148)
XLA Ops:
  0.0 0.7 and_select_fusion.1
  0.7 0.2 convert_reduce_fusion
  0.9 0.2 select_reduce_fusion
  1.0 0.1 select_n.32
  1.2 79.4 %spread.1 = (bf16[4,64,3,32,128]{4,3,2,1,0:T(8,128)(2,1)S(1)}, bf16[64,8,64,128]{3,2,1,0:T(8,128)(2,1)S(1)}, s32[64,1,128]{2,1,0:T(1,128)S(1)}) custom-call(s32[192]{0:T(256)S(1)} %get-tuple-element.12.source, s32[64,1,128]{2,1,0:T(1,128)S(1)} %bitcast.6, bf16[128,128,128]{2,1,0:T(8,128)(2,1)} %footprints.1, bf16[64,1024]{1,0:T(8,128)(2,1)} %prior_h.1), custom_call_target="tpu_custom_call" | custom-call | tf_op jit(solution)/shard_map/spread/pallas_call | solution.py:280
  80.5 16.3 %local.1 = bf16[512,64,128]{2,1,0:T(8,128)(2,1)S(1)} custom-call(s32[64,1,128]{2,1,0:T(1,128)S(1)} %get-tuple-element.8.codes, bf16[4,64,3,32,128]{4,3,2,1,0:T(8,128)(2,1)S(1)} %get-tuple-element.9.tiles, bf16[512,64,128]{2,1,0:T(8,128)(2,1)S(1)} %bitcast.5, f32[64,2048]{1,0:T(8,128)} %observed_h.1, s32[16,1,128]{2,1,0:T(1,128)} %bitcast.7), custom_call_target="tpu_custom_call" | custom-call | tf_op jit(solution)/shard_map/local/pallas_call | solution.py:367
  96.9 37.1 %gather.1 = f32[64,1024]{1,0:T(8,128)S(1)} custom-call(bf16[8,4,2,8,64,128]{5,4,3,2,1,0:T(8,128)(2,1)S(1)} %bitcast.4), custom_call_target="tpu_custom_call" | custom-call | tf_op jit(solution)/shard_map/gather/pallas_call | solution.py:595
  134.0 0.7 copy.8
  (3 shorter events, 0.0 us)

commit v4 on v3

--- a/solution.py
+++ b/solution.py
@@ -33,6 +33,18 @@
     return source, coded
 
 
+SPREAD_ORDER = (
+    ("T", 0), ("T", 1), ("T", 7), ("A0",), ("T", 2), ("T", 6), ("Y1", 0), ("Y1", 1), ("Y1", 7), ("Z", 0, 1),
+    ("Z", 1, 1), ("X", 0, 0), ("X", 1, 0), ("Y2", 0, 0), ("Y2", 1, 0), ("T", 3), ("T", 5), ("Y2", 0, 1),
+    ("Y2", 1, 1), ("X", 0, 7), ("X", 1, 7), ("Y1", 2), ("Y1", 6), ("Y2", 0, 7), ("Y2", 1, 7), ("X", 0, 1),
+    ("Z", 0, 2), ("X", 1, 1), ("Z", 1, 2), ("XL", 0), ("T", 4), ("XL", 7), ("Y2", 0, 2), ("Y2", 1, 2),
+    ("X", 1, 6), ("X", 0, 6), ("XL", 1), ("Y2", 0, 6), ("Y2", 1, 6), ("Y1", 3), ("X", 0, 2), ("X", 1, 2),
+    ("Y1", 5), ("Z", 0, 3), ("Z", 1, 3), ("XL", 6), ("XL", 2), ("X", 0, 5), ("X", 1, 5), ("Y2", 0, 3),
+    ("Y2", 1, 3), ("X", 0, 3), ("X", 1, 3), ("XL", 5), ("Y1", 4), ("Z", 0, 4), ("Y2", 0, 5), ("Y2", 1, 5),
+    ("XL", 3), ("X", 0, 4), ("X", 1, 4), ("Y2", 0, 4), ("Y2", 1, 4), ("XL", 4),
+)
+
+
 def spread_kernel(
     source, coded, footprints, prior_h, tiles, anoms, codes,
     prior, quarter, staged, sums, shard,
@@ -132,15 +144,11 @@
         go(remote(group(q, dz), group(q, dz), s_y.at[0, dz], r_y.at[0, dz], mem=at_y(1)))
         go(remote(group(q, dz), group(q, dz), s_y.at[1, dz], r_y.at[1, dz], mem=at_y(-1)))
 
-    def y_second(dz):
-        back = group(at_y(-1), dz)
-        wait_for(back, r_y.at[0, dz])
-        part = group(at_y(-1), dz, 0, 4)
-        go(remote(part, part, s_y.at[2, dz], r_y2.at[0, dz], mem=at_y(1)))
-        fore = group(at_y(1), dz)
-        wait_for(fore, r_y.at[1, dz])
-        part = group(at_y(1), dz, 4, 4)
-        go(remote(part, part, s_y.at[3, dz], r_y2.at[1, dz], mem=at_y(-1)))
+    def y_second(i, dz):
+        from_, to = ((-1, 1), (1, -1))[i]
+        wait_for(group(at_y(from_), dz), r_y.at[i, dz])
+        half = group(at_y(from_), dz, 4 * i, 4)
+        go(remote(half, half, s_y.at[2 + i, dz], r_y2.at[i, dz], mem=at_y(to)))
 
     def y_last(dz):
         wait_for(group(at_y(2), dz, 0, 4), r_y2.at[0, dz])
@@ -165,18 +173,14 @@
         go(remote(src, b, s_x.at[1, k], r_x.at[1, k], tile=index(z, at_x(-1), core)))
         go(remote(src, b, s_sib.at[0, k], r_sib.at[0, k], tile=index(z, x, 1 - core)))
 
-    def x_second(oz):
+    def x_second(i, oz):
         k = oz % NZ
-        b = block(oz, -1)
-        wait_for(b, r_x.at[0, k])
-        h = b.at[pl.ds(0, 4)]
-        go(remote(h, h, s_x.at[2, k], r_x2.at[0, k], tile=index(z, at_x(1), core)))
-        to_sibling(oz, -1)
-        b = block(oz, 1)
-        wait_for(b, r_x.at[1, k])
-        h = b.at[pl.ds(4, 4)]
-        go(remote(h, h, s_x.at[3, k], r_x2.at[1, k], tile=index(z, at_x(-1), core)))
-        to_sibling(oz, 1)
+        from_, to = ((-1, 1), (1, -1))[i]
+        b = block(oz, from_)
+        wait_for(b, r_x.at[i, k])
+        h = b.at[pl.ds(4 * i, 4)]
+        go(remote(h, h, s_x.at[2 + i, k], r_x2.at[i, k], tile=index(z, at_x(to), core)))
+        to_sibling(oz, from_)
 
     def x_last(oz):
         k = oz % NZ
@@ -185,81 +189,37 @@
         wait_for(b.at[pl.ds(4, 4)], r_x2.at[1, k])
         to_sibling(oz, 2)
 
-    def z_step(k):
-        up, down = index(at_z(1), x, core), index(at_z(-1), x, core)
+    def z_step(i, k):
         if k < 4:
-            b = block(-k, 0)
-            wait_for(b, r_z.at[0, k])
-            h = b if k < 3 else b.at[pl.ds(0, 4)]
-            go(remote(h, h, s_z.at[0, k + 1], r_z.at[0, k + 1], tile=up))
-            x_first(-k)
-            b = block(k, 0)
-            wait_for(b, r_z.at[1, k])
-            h = b if k < 3 else b.at[pl.ds(4, 4)]
-            go(remote(h, h, s_z.at[1, k + 1], r_z.at[1, k + 1], tile=down))
-            x_first(k)
+            b = block((-k, k)[i], 0)
+            wait_for(b, r_z.at[i, k])
+            h = b if k < 3 else b.at[pl.ds(4 * i, 4)]
+            go(remote(h, h, s_z.at[i, k + 1], r_z.at[i, k + 1], tile=index(at_z((1, -1)[i]), x, core)))
+            x_first((-k, k)[i])
         else:
             b = block(4, 0)
             wait_for(b.at[pl.ds(0, 4)], r_z.at[0, 4])
             wait_for(b.at[pl.ds(4, 4)], r_z.at[1, 4])
             x_first(4)
 
-    send_tiles(0)
-
-    for cp in sum_sends:
-        cp.wait()
-    mean = (sums[0] + sums[1] + sums[2] + sums[3]) / MEMBERS
-    for j in range(FLUX_DEV):
-        shard[j] = (prior[:, j * B : (j + 1) * B].astype(F32) - mean[j : j + 1, :]).astype(BF16)
     own_copy = pltpu.make_async_copy(shard, anoms.at[me], s_local)
-    own_copy.start()
-    go(remote(shard, anoms.at[me], s_z.at[0, 1], r_z.at[0, 1], tile=index(at_z(1), x, core)))
-    go(remote(shard, anoms.at[me], s_z.at[1, 1], r_z.at[1, 1], tile=index(at_z(-1), x, core)))
-    x_first(0, shard)
-
-    send_tiles(1)
-    send_tiles(7)
-    y_first(0)
-    z_step(1)
-    send_tiles(2)
-    send_tiles(6)
-    x_second(0)
-    y_first(1)
-    y_first(7)
-    z_step(2)
-    send_tiles(3)
-    send_tiles(5)
-    y_second(0)
-    x_second(-1)
-    x_second(1)
-    z_step(3)
-    send_tiles(4)
-    y_second(1)
-    y_second(7)
-    y_first(2)
-    y_first(6)
-    x_last(0)
-    x_second(-2)
-    x_second(2)
-    z_step(4)
-    y_first(3)
-    y_first(5)
-    y_second(2)
-    y_second(6)
-    x_last(-1)
-    x_last(1)
-    x_second(-3)
-    x_second(3)
-    y_first(4)
-    y_second(3)
-    y_second(5)
-    x_last(-2)
-    x_last(2)
-    x_second(4)
-    y_second(4)
-    x_last(-3)
-    x_last(3)
-    x_last(4)
+
+    def send_shard():
+        for cp in sum_sends:
+            cp.wait()
+        mean = (sums[0] + sums[1] + sums[2] + sums[3]) / MEMBERS
+        for j in range(FLUX_DEV):
+            shard[j] = (prior[:, j * B : (j + 1) * B].astype(F32) - mean[j : j + 1, :]).astype(BF16)
+        own_copy.start()
+        go(remote(shard, anoms.at[me], s_z.at[0, 1], r_z.at[0, 1], tile=index(at_z(1), x, core)))
+        go(remote(shard, anoms.at[me], s_z.at[1, 1], r_z.at[1, 1], tile=index(at_z(-1), x, core)))
+        x_first(0, shard)
+
+    acts = {
+        "T": send_tiles, "A0": send_shard, "Z": z_step, "X": x_second, "XL": x_last, "Y1": y_first, "Y2": y_second
+    }
+    for name, *numbers in SPREAD_ORDER:
+        acts[name](*numbers)
     for dz in (0, 1, 7, 2, 6, 3, 5, 4):
         y_last(dz)
     for oz in (0, 1, 7, 2, 6, 3, 5, 4):
@@ -313,7 +273,7 @@
     weight_in = pltpu.make_async_copy(weight_h, weight, s_weight)
     weight_in.start()
     modelled[...] = jnp.zeros_like(modelled)
-    step = 2
+    step = 16
 
     def fetch(i, o, s):
         src = i * step + o
@@ -330,7 +290,7 @@
                     anoms[col], tile, (((1,), (1,)), ((), ())), preferred_element_type=F32
                 )
                 terms.append((row, term))
-        total[pl.ds(i * 16, 16)] = jnp.zeros((16, LM, B), F32)
+        total[pl.ds(i * 128, 128)] = jnp.zeros((128, LM, B), F32)
         for row, term in terms:
             modelled[row] += term
 
@@ -570,18 +530,15 @@
                 wait_for(xb2.at[i], r_xb.at[i, 1])
             result(NA, [*sources, xb2.at[0], xb2.at[1]], NB)
 
-    events = []
-    for k in range(2):
-        events.append((1.9 + 0.3 * k, b_far, (k,)))
-    for k in range(4):
-        events.append((2.0 + 0.3 * k, a_far, (k,)))
+    events = [(5.0, b_far, (k,)) for k in range(2)] + [(5.1, a_far, (k,)) for k in range(4)]
     for j in range(8):
-        events.append((4.0 + 1.7 * (j // 2 + 1), a_near, (j,)))
-        events.append((11.2 + 1.65 * (j + 1), a_own, (NEAR_X[j],)))
+        events.append((8.3 + 1.65 * (j // 2), a_near, (j,)))
+    for oz, when in ((4, 14.9), (5, 18.2), (3, 18.2), (6, 21.5), (2, 21.6), (7, 24.9), (1, 24.9), (0, 28.2)):
+        events.append((when, a_own, (oz,)))
     for j in range(4):
-        for step in (1, 2, 3):
-            events.append((4.0 * step + min(j + 1, 2 if step == 1 else 4), b_near, (step, j)))
-    for ox, when in ((2, 17.0), (1, 19.5), (3, 19.6), (0, 22.5)):
+        for step, when in ((1, min(7.7 + j, 8.7)), (2, 10.4 + j), (3, 13.1 + j)):
+            events.append((when, b_near, (step, j)))
+    for ox, when in ((2, 18.6), (1, 23.0), (3, 23.1), (0, 28.5)):
         events.append((when, b_own, (ox,)))
     for _, act, args in sorted(events, key=lambda e: e[0]):
         act(*args)

time: 135 us -> 123 us (0.911)
  Pallas kernels: 133 us -> 121 us
    pallas_call x1, Pallas kernels: 16.3 us -> 9.76 us  [local(): pl.pallas_call(local_kernel, out_shape=jax.ShapeDtypeStruct((NT * FLUX_DE...]
    pallas_call x1, Pallas kernels: 79.4 us -> 76.1 us  [spread(): pl.pallas_call(spread_kernel, out_shape=(jax.ShapeDtypeStruct((NY, NT, CA...]
    pallas_call x1, Pallas kernels: 37.1 us -> 34.8 us  [gather(): pl.pallas_call(gather_kernel, out_shape=jax.ShapeDtypeStruct((LM, FLUX_DE...]
where the time goes in v4:
time: 123 us
  Pallas kernels  121 us (98%)
    pallas_call x1, Pallas kernels, spread(): pl.pallas_call(spread_kernel, out_shape=(jax.ShapeDtypeStruct((NY, NT, CA...  76.1 us
    pallas_call x1, Pallas kernels, gather(): pl.pallas_call(gather_kernel, out_shape=jax.ShapeDtypeStruct((LM, FLUX_DE...  34.8 us
    pallas_call x1, Pallas kernels, local(): pl.pallas_call(local_kernel, out_shape=jax.ShapeDtypeStruct((NT * FLUX_DE...  9.76 us

profile of v4, /device:TPU:8, one launch (start us, length us, event | category | flops | bytes accessed | tf_op | source)
XLA Modules:
  0.0 122.5 jit_solution(14035784224197000694)
XLA Ops:
  0.0 0.7 and_select_fusion.1
  0.7 0.2 convert_reduce_fusion
  0.9 0.2 select_reduce_fusion
  1.0 0.1 select_n.32
  1.2 76.1 %spread.1 = (bf16[4,64,3,32,128]{4,3,2,1,0:T(8,128)(2,1)S(1)}, bf16[64,8,64,128]{3,2,1,0:T(8,128)(2,1)S(1)}, s32[64,1,128]{2,1,0:T(1,128)S(1)}) custom-call(s32[192]{0:T(256)S(1)} %get-tuple-element.12.source, s32[64,1,128]{2,1,0:T(1,128)S(1)} %bitcast.6, bf16[128,128,128]{2,1,0:T(8,128)(2,1)} %footprints.1, bf16[64,1024]{1,0:T(8,128)(2,1)} %prior_h.1), custom_call_target="tpu_custom_call" | custom-call | tf_op jit(solution)/shard_map/spread/pallas_call | solution.py:240
  77.2 9.8 %local.1 = bf16[512,64,128]{2,1,0:T(8,128)(2,1)S(1)} custom-call(s32[64,1,128]{2,1,0:T(1,128)S(1)} %get-tuple-element.8.codes, bf16[4,64,3,32,128]{4,3,2,1,0:T(8,128)(2,1)S(1)} %get-tuple-element.9.tiles, bf16[512,64,128]{2,1,0:T(8,128)(2,1)S(1)} %bitcast.5, f32[64,2048]{1,0:T(8,128)} %observed_h.1, s32[16,1,128]{2,1,0:T(1,128)} %bitcast.7), custom_call_target="tpu_custom_call" | custom-call | tf_op jit(solution)/shard_map/local/pallas_call | solution.py:327
  87.0 34.8 %gather.1 = f32[64,1024]{1,0:T(8,128)S(1)} custom-call(bf16[8,4,2,8,64,128]{5,4,3,2,1,0:T(8,128)(2,1)S(1)} %bitcast.4), custom_call_target="tpu_custom_call" | custom-call | tf_op jit(solution)/shard_map/gather/pallas_call | solution.py:552
  121.8 0.7 copy.8
  (3 shorter events, 0.0 us)

commit v5 on v4

--- a/solution.py
+++ b/solution.py
@@ -18,18 +18,27 @@
 F32, BF16 = jnp.float32, jnp.bfloat16
 
 
-def route(tile_row, tile_col):
-    count = tile_row.shape[0]
-    owner = tile_row // SOUND_DEV
-    position = jnp.arange(count)
-    earlier = (owner[:, None] == owner[None, :]) & (position[None, :] < position[:, None])
-    slot = owner * CAP + jnp.sum(earlier.astype(jnp.int32), axis=1)
-    match = slot[None, :] == jnp.arange(NT * CAP)[:, None]
-    source = jnp.sum(jnp.where(match, position[None, :], 0), axis=1)
-    blocks = (tile_row % SOUND_DEV) * 512 + tile_col
-    coded = jnp.sum(jnp.where(match, blocks[None, :] + 1, 0), axis=1)
-    coded = jnp.where(coded == 0, SOUND_DEV * 512, coded - 1)
-    coded = jnp.pad(coded.reshape(NT, CAP), ((0, 0), (0, B - CAP))).reshape(NT, 1, B)
+def route(row, col):
+    shape = (B, B)
+    down, across = lax.broadcasted_iota(jnp.int32, shape, 0), lax.broadcasted_iota(jnp.int32, shape, 1)
+
+    def column(v):
+        return jnp.sum(jnp.where(down == across, v, 0), axis=1, keepdims=True)
+
+    owner = row // SOUND_DEV
+    earlier = (column(owner) == owner) & (down < across)
+    place = jnp.sum(earlier.astype(jnp.int32), axis=0, keepdims=True)
+    slot = column(owner * CAP + place)
+    index = lax.broadcasted_iota(jnp.int32, (B, 2 * B), 0)
+    at = lax.broadcasted_iota(jnp.int32, (B, 2 * B), 1)
+    source = jnp.sum(jnp.where(slot == at, index, 0), axis=0, keepdims=True)
+    blocks = (row - owner * SOUND_DEV) * 512 + col - SOUND_DEV * 512
+    mine = lax.broadcasted_iota(jnp.int32, (NT, B), 0) == owner
+    lane = lax.broadcasted_iota(jnp.int32, (NT, B), 1)
+    coded = jnp.full((NT, B), SOUND_DEV * 512, jnp.int32)
+    for k in range(CAP):
+        found = jnp.sum(jnp.where(mine & (place == k), blocks, 0), axis=1, keepdims=True)
+        coded = coded + jnp.where(lane == k, found, 0)
     return source, coded
 
 
@@ -46,10 +55,10 @@
 
 
 def spread_kernel(
-    source, coded, footprints, prior_h, tiles, anoms, codes,
-    prior, quarter, staged, sums, shard,
-    s_fp, s_prior, s_sum, r_sum, s_tile, r_tile, s_code, r_code, s_y, r_y, r_y2,
-    s_local, s_z, r_z, s_x, r_x, r_x2, s_sib, r_sib,
+    row_h, col_h, footprints, prior_h, tiles, anoms, codes,
+    row, col, source_v, source, coded, prior, quarter, staged, sums, shard,
+    s_row, s_fp, s_prior, s_sum, r_sum, s_tile, r_tile, s_code, r_code, s_y, r_y, r_y2,
+    s_local, s_z, r_z, s_x, r_x, r_x2, s_sib, r_sib, came,
 ):
     me = lax.axis_index("tile")
     q = lax.axis_index("mem")
@@ -79,6 +88,10 @@
     def wait_for(ref, sem):
         pltpu.make_async_copy(ref, ref, sem).wait()
 
+    row_copy = pltpu.make_async_copy(row_h, row, s_row.at[0])
+    row_copy.start()
+    col_copy = pltpu.make_async_copy(col_h, col, s_row.at[1])
+    col_copy.start()
     prior_copy = pltpu.make_async_copy(prior_h, prior, s_prior)
     prior_copy.start()
     fp_copy = pltpu.make_async_copy(
@@ -87,23 +100,41 @@
     fp_copy.start()
 
     barrier = pltpu.get_barrier_semaphore()
-
-    @pl.loop(1, NT)
-    def _(o):
+    for o in range(1, 8):
         pl.semaphore_signal(
-            barrier, inc=1, device_id={"tile": lax.rem(me + o, NT), "mem": q}, device_id_type=MESH
+            barrier, inc=1, device_id={"tile": z * 8 + lax.rem(me + o, 8), "mem": q}, device_id_type=MESH
         )
-
     for o in range(1, NY):
+        pl.semaphore_signal(barrier, inc=1, device_id={"tile": me, "mem": at_y(o)}, device_id_type=MESH)
+    for o in (1, -1):
         pl.semaphore_signal(
-            barrier, inc=1, device_id={"tile": me, "mem": at_y(o)}, device_id_type=MESH
+            barrier, inc=1, device_id={"tile": index(at_z(o), x, core), "mem": q}, device_id_type=MESH
         )
 
+    def tell(stage):
+        for i, o in enumerate((1, -1)):
+            pl.semaphore_signal(
+                came.at[i, stage], inc=1, device_id={"tile": index(at_z(o), x, core), "mem": q}, device_id_type=MESH
+            )
+
+    def hear(stage):
+        for i in range(2):
+            pl.semaphore_wait(came.at[i, stage], 1)
+
+    row_copy.wait()
+    col_copy.wait()
+    source_row, coded_rows = route(row[...], col[...])
+    source_v[...] = source_row
+    source_copy = pltpu.make_async_copy(source_v, source, s_row.at[2])
+    source_copy.start()
+    for t in range(NT):
+        coded[t] = coded_rows[t : t + 1]
     prior_copy.wait()
     for j in range(FLUX_DEV):
         part = jnp.sum(prior[:, j * B : (j + 1) * B].astype(F32), axis=0, keepdims=True)
         sums[0, j : j + 1, :] = part
-    pl.semaphore_wait(barrier, NT - 1 + NY - 1)
+    pl.semaphore_wait(barrier, 7 + NY - 1 + 2)
+    tell(1)
 
     sum_sends = []
     for o in range(1, NY):
@@ -111,21 +142,26 @@
         cp.start()
         sum_sends.append(cp)
     fp_copy.wait()
+    source_copy.wait()
 
     def send_tiles(dz):
         first = 1 if dz == 0 else 0
+        if 1 <= dz <= 4:
+            hear(dz)
+            if dz < 4:
+                tell(dz + 1)
 
         @pl.loop(first, 8)
         def _(o):
             t = at_z(dz) * 8 + lax.rem(me + o, 8)
             for s in range(CAP):
-                staged[t, s] = quarter[source[t * CAP + s]]
+                staged[t, s] = quarter[source[0, t * CAP + s]]
             remote(staged.at[t], tiles.at[q, me], s_tile, r_tile.at[dz], tile=t).start()
             remote(coded.at[t], codes.at[me], s_code, r_code, tile=t).start()
 
         if dz == 0:
             for s in range(CAP):
-                staged[me, s] = quarter[source[me * CAP + s]]
+                staged[me, s] = quarter[source[0, me * CAP + s]]
             pltpu.make_async_copy(staged.at[me], tiles.at[q, me], r_tile.at[0]).start()
             pltpu.make_async_copy(coded.at[me], codes.at[me], r_code).start()
 
@@ -219,6 +255,8 @@
         "T": send_tiles, "A0": send_shard, "Z": z_step, "X": x_second, "XL": x_last, "Y1": y_first, "Y2": y_second
     }
     for name, *numbers in SPREAD_ORDER:
+        while len(pending) > 40:
+            pending.pop(0).wait_send()
         acts[name](*numbers)
     for dz in (0, 1, 7, 2, 6, 3, 5, 4):
         y_last(dz)
@@ -233,7 +271,7 @@
     wait_for(codes.at[pl.ds(0, NT - 1)], s_code)
 
 
-def spread(source, coded, footprints, prior):
+def spread(tile_row, tile_col, footprints, prior):
     hbm = pl.BlockSpec(memory_space=pltpu.HBM)
     vmem = pl.BlockSpec(memory_space=pltpu.VMEM)
     dma = pltpu.SemaphoreType.DMA
@@ -244,24 +282,29 @@
             jax.ShapeDtypeStruct((NT, FLUX_DEV, LM, B), BF16),
             jax.ShapeDtypeStruct((NT, 1, B), jnp.int32),
         ),
-        in_specs=[pl.BlockSpec(memory_space=pltpu.SMEM), vmem, hbm, hbm],
+        in_specs=[hbm, hbm, hbm, hbm],
         out_specs=(vmem, vmem, vmem),
         scratch_shapes=[
+            pltpu.VMEM((1, B), jnp.int32),
+            pltpu.VMEM((1, B), jnp.int32),
+            pltpu.VMEM((1, 2 * B), jnp.int32),
+            pltpu.SMEM((1, 2 * B), jnp.int32),
+            pltpu.VMEM((NT, 1, B), jnp.int32),
             pltpu.VMEM((LM, FLUX_DEV * B), BF16),
             pltpu.VMEM((B, 32, B), BF16),
             pltpu.VMEM((NT, CAP, 32, B), BF16),
             pltpu.VMEM((NY, FLUX_DEV, B), F32),
             pltpu.VMEM((FLUX_DEV, LM, B), BF16),
-            dma, dma, dma((NY,)), dma((NY,)), dma, dma((NZ,)), dma, dma,
+            dma((3,)), dma, dma, dma((NY,)), dma((NY,)), dma, dma((NZ,)), dma, dma,
             dma((4, NZ)), dma((2, NZ)), dma((2, NZ)),
             dma, dma((2, 5)), dma((2, 5)), dma((4, NZ)), dma((2, NZ)), dma((2, NZ)),
-            dma((NX, NZ)), dma((NX, NZ)),
+            dma((NX, NZ)), dma((NX, NZ)), pltpu.SemaphoreType.REGULAR((2, 5)),
         ],
         compiler_params=pltpu.CompilerParams(
             collective_id=0, has_side_effects=True, vmem_limit_bytes=16 * 2**20
         ),
         name="spread",
-    )(source, coded, footprints, prior)
+    )(tile_row, tile_col, footprints, prior)
 
 
 def local_kernel(
@@ -353,7 +396,7 @@
 def gather_kernel(
     part, out,
     pa, pb, ra, rb, xa1, xa2, zb1, zb2, za1, za2, xb1, xb2,
-    s_sib_a, r_sib_a, s_sib_b, r_sib_b,
+    s_sib_a, r_sib_a, s_sib_b, r_sib_b, s_a2, r_a2, s_b4, r_b4,
     s_xa1, r_xa1, s_xa2, r_xa2, s_zb1, r_zb1, s_zb2, r_zb2, s_za, r_za, s_xb, r_xb,
 ):
     me = lax.axis_index("tile")
@@ -393,8 +436,13 @@
         pl.semaphore_signal(barrier, inc=1, device_id={"tile": t, "mem": q}, device_id_type=MESH)
     pl.semaphore_wait(barrier, 5)
 
-    for kind, d in (("b", 4), ("a", 2), ("b", 3), ("b", 5), ("a", 1), ("a", 3),
-                    ("b", 2), ("b", 6), ("b", 1), ("b", 7), ("a", 0), ("b", 0)):
+    for ox in NEAR_Z:
+        xx = at_x(ox)
+        send(part.at[at_z(4), xx, 1 - core, pl.ds(NA, NB)], rb.at[4, xx], s_b4.at[ox], r_b4.at[ox], sibling)
+    for oz in NEAR_X:
+        zz = at_z(oz)
+        send(part.at[zz, at_x(2), 1 - core, pl.ds(0, NA)], ra.at[2, zz], s_a2.at[oz], r_a2.at[oz], sibling)
+    for kind, d in (("b", 3), ("b", 5), ("a", 1), ("a", 3), ("b", 2), ("b", 6), ("b", 1), ("b", 7), ("a", 0), ("b", 0)):
         if kind == "a":
             send(part.at[:, at_x(d), 1 - core, pl.ds(0, NA)], ra.at[d], s_sib_a.at[d], r_sib_a.at[d], sibling)
         else:
@@ -405,13 +453,15 @@
     def from_a(d, zz):
         if ("a", d) not in settled:
             settled.add(("a", d))
-            wait_for(ra.at[d], r_sib_a.at[d])
+            if d != 2:
+                wait_for(ra.at[d], r_sib_a.at[d])
         return [part.at[zz, at_x(d), core], ra.at[d, zz]]
 
     def from_b(d, xx):
         if ("b", d) not in settled:
             settled.add(("b", d))
-            wait_for(rb.at[d], r_sib_b.at[d])
+            if d != 4:
+                wait_for(rb.at[d], r_sib_b.at[d])
         return [part.at[at_z(d), xx, core, pl.ds(NA, NB)], rb.at[d, xx]]
 
     def total(dst, sources, first, last):
@@ -435,6 +485,7 @@
     def a_far(k):
         for i in range(2):
             zz = at_z(FAR_X[i][k])
+            wait_for(ra.at[2, zz], r_a2.at[FAR_X[i][k]])
             total(pa.at[2, zz], from_a(2, zz), 0, NA)
             send(pa.at[2, zz], xa1.at[i, k], s_xa1.at[i, k], r_xa1.at[i, k], x_next[i])
 
@@ -485,6 +536,7 @@
     def b_far(k):
         for i in range(2):
             xx = at_x(FAR_Z[i][k])
+            wait_for(rb.at[4, xx], r_b4.at[FAR_Z[i][k]])
             total(pb.at[4, xx], from_b(4, xx), 0, NB)
             send(pb.at[4, xx], zb1.at[i, k], s_zb1.at[i, k], r_zb1.at[i, k], z_next[i])
 
@@ -541,6 +593,8 @@
     for ox, when in ((2, 18.6), (1, 23.0), (3, 23.1), (0, 28.5)):
         events.append((when, b_own, (ox,)))
     for _, act, args in sorted(events, key=lambda e: e[0]):
+        while len(pending) > 30:
+            pending.pop(0).wait_send()
         act(*args)
     for cp in pending:
         cp.wait_send()
@@ -567,7 +621,7 @@
             pltpu.VMEM((2, 3, NA, LM, B), BF16),
             pltpu.VMEM((NB, LM, B), BF16),
             pltpu.VMEM((2, NB, LM, B), BF16),
-            dma((NX,)), dma((NX,)), dma((NZ,)), dma((NZ,)),
+            dma((NX,)), dma((NX,)), dma((NZ,)), dma((NZ,)), dma((NZ,)), dma((NZ,)), dma((NX,)), dma((NX,)),
             dma((2, 4)), dma((2, 4)), dma((2, NZ)), dma((2, NZ)),
             dma((2, 2)), dma((2, 2)), dma((2, 3, NX)), dma((2, 3, NX)),
             dma((2, 4)), dma((2, 4)), dma((2, 2)), dma((2, 2)),
@@ -582,8 +636,8 @@
 def body(footprints, tile_row, tile_col, prior_flux, observed, precision_weight):
     pin = functools.partial(pltpu.with_memory_space_constraint, memory_space=pltpu.HBM)
     footprints, prior_flux, observed = pin(footprints), pin(prior_flux), pin(observed)
-    source, coded = route(tile_row, tile_col)
-    tiles, anoms, codes = spread(source, coded, footprints, prior_flux)
+    tile_row, tile_col = pin(tile_row.reshape(1, B)), pin(tile_col.reshape(1, B))
+    tiles, anoms, codes = spread(tile_row, tile_col, footprints, prior_flux)
     weight = pin(precision_weight.reshape(SOUND_DEV, 1, B))
     part = local(codes, tiles, anoms, observed, weight)
     return gather(part)

time: 123 us -> 121 us (0.984)
  Pallas kernels: 121 us -> 119 us
    pallas_call x1, Pallas kernels: 76.1 us -> 71.2 us  [spread(): pl.pallas_call(spread_kernel, out_shape=(jax.ShapeDtypeStruct((NY, NT, CA...]
    pallas_call x1, Pallas kernels: 34.8 us -> 38.2 us  [gather(): pl.pallas_call(gather_kernel, out_shape=jax.ShapeDtypeStruct((LM, FLUX_DE...]
where the time goes in v5:
time: 121 us; the launch traced here: 120 us
  Pallas kernels  119 us (98%)
    pallas_call x1, Pallas kernels, spread(): pl.pallas_call(spread_kernel, out_shape=(jax.ShapeDtypeStruct((NY, NT, CA...  71.2 us
    pallas_call x1, Pallas kernels, gather(): pl.pallas_call(gather_kernel, out_shape=jax.ShapeDtypeStruct((LM, FLUX_DE...  38.2 us
    pallas_call x1, Pallas kernels, local(): pl.pallas_call(local_kernel, out_shape=jax.ShapeDtypeStruct((NT * FLUX_DE...  9.75 us

profile of v5, /device:TPU:8, one launch (start us, length us, event | category | flops | bytes accessed | tf_op | source)
XLA Modules:
  0.0 119.9 jit_solution(12592404722138102363)
XLA Ops:
  0.0 71.2 %spread.1 = (bf16[4,64,3,32,128]{4,3,2,1,0:T(8,128)(2,1)S(1)}, bf16[64,8,64,128]{3,2,1,0:T(8,128)(2,1)S(1)}, s32[64,1,128]{2,1,0:T(1,128)S(1)}) custom-call(s32[1,128]{1,0:T(1,128)} %bitcast.8, s32[1,128]{1,0:T(1,128)} %bitcast.9, bf16[128,128,128]{2,1,0:T(8,128)(2,1)} %footprints.1, bf16[64,1024]{1,0:T(8,128)(2,1)} %prior_h.1), custom_call_target="tpu_custom_call" | custom-call | tf_op jit(solution)/shard_map/spread/pallas_call | solution.py:278
  71.2 9.8 %local.1 = bf16[512,64,128]{2,1,0:T(8,128)(2,1)S(1)} custom-call(s32[64,1,128]{2,1,0:T(1,128)S(1)} %get-tuple-element.8.codes, bf16[4,64,3,32,128]{4,3,2,1,0:T(8,128)(2,1)S(1)} %get-tuple-element.9.tiles, bf16[512,64,128]{2,1,0:T(8,128)(2,1)S(1)} %bitcast.6, f32[64,2048]{1,0:T(8,128)} %observed_h.1, s32[16,1,128]{2,1,0:T(1,128)} %bitcast.7), custom_call_target="tpu_custom_call" | custom-call | tf_op jit(solution)/shard_map/local/pallas_call | solution.py:370
  81.0 38.2 %gather.1 = f32[64,1024]{1,0:T(8,128)S(1)} custom-call(bf16[8,4,2,8,64,128]{5,4,3,2,1,0:T(8,128)(2,1)S(1)} %bitcast.5), custom_call_target="tpu_custom_call" | custom-call | tf_op jit(solution)/shard_map/gather/pallas_call | solution.py:606
  119.2 0.7 copy.8

commit v6 on v5

--- a/solution.py
+++ b/solution.py
@@ -43,13 +43,13 @@
 
 
 SPREAD_ORDER = (
-    ("T", 0), ("T", 1), ("T", 7), ("A0",), ("T", 2), ("T", 6), ("Y1", 0), ("Y1", 1), ("Y1", 7), ("Z", 0, 1),
-    ("Z", 1, 1), ("X", 0, 0), ("X", 1, 0), ("Y2", 0, 0), ("Y2", 1, 0), ("T", 3), ("T", 5), ("Y2", 0, 1),
-    ("Y2", 1, 1), ("X", 0, 7), ("X", 1, 7), ("Y1", 2), ("Y1", 6), ("Y2", 0, 7), ("Y2", 1, 7), ("X", 0, 1),
-    ("Z", 0, 2), ("X", 1, 1), ("Z", 1, 2), ("XL", 0), ("T", 4), ("XL", 7), ("Y2", 0, 2), ("Y2", 1, 2),
-    ("X", 1, 6), ("X", 0, 6), ("XL", 1), ("Y2", 0, 6), ("Y2", 1, 6), ("Y1", 3), ("X", 0, 2), ("X", 1, 2),
-    ("Y1", 5), ("Z", 0, 3), ("Z", 1, 3), ("XL", 6), ("XL", 2), ("X", 0, 5), ("X", 1, 5), ("Y2", 0, 3),
-    ("Y2", 1, 3), ("X", 0, 3), ("X", 1, 3), ("XL", 5), ("Y1", 4), ("Z", 0, 4), ("Y2", 0, 5), ("Y2", 1, 5),
+    ("T", 0), ("T", 1), ("T", 7), ("A0",), ("T", 2), ("T", 6), ("Y1", 0), ("Y1", 1), ("Y1", 7), ("Y2", 0, 0),
+    ("Y2", 1, 0), ("Z", 0, 1), ("X", 0, 0), ("X", 1, 0), ("Z", 1, 1), ("Y2", 0, 1), ("Y2", 1, 1), ("T", 3),
+    ("T", 5), ("X", 0, 7), ("X", 1, 7), ("Y2", 0, 7), ("Y2", 1, 7), ("Y1", 2), ("Y1", 6), ("XL", 0),
+    ("Z", 0, 2), ("X", 0, 1), ("X", 1, 1), ("Z", 1, 2), ("T", 4), ("XL", 7), ("Y2", 0, 2), ("Y2", 1, 2),
+    ("X", 0, 6), ("X", 1, 6), ("XL", 1), ("Y2", 0, 6), ("Y2", 1, 6), ("X", 0, 2), ("X", 1, 2), ("Y1", 3),
+    ("Y1", 5), ("Z", 0, 3), ("Z", 1, 3), ("XL", 6), ("XL", 2), ("Y2", 0, 3), ("Y2", 1, 3), ("X", 0, 5),
+    ("X", 1, 5), ("X", 0, 3), ("X", 1, 3), ("Y2", 0, 5), ("Y2", 1, 5), ("Y1", 4), ("Z", 0, 4), ("XL", 5),
     ("XL", 3), ("X", 0, 4), ("X", 1, 4), ("Y2", 0, 4), ("Y2", 1, 4), ("XL", 4),
 )
 
@@ -57,8 +57,8 @@
 def spread_kernel(
     row_h, col_h, footprints, prior_h, tiles, anoms, codes,
     row, col, source_v, source, coded, prior, quarter, staged, sums, shard,
-    s_row, s_fp, s_prior, s_sum, r_sum, s_tile, r_tile, s_code, r_code, s_y, r_y, r_y2,
-    s_local, s_z, r_z, s_x, r_x, r_x2, s_sib, r_sib, came,
+    s_row, s_fp, s_prior, s_sum, r_sum, s_tile, r_tile, s_code, r_code, s_y, r_y, s_y2, r_y2,
+    s_local, s_z, r_z, s_x, r_x, s_x2, r_x2, s_sib, r_sib, came,
 ):
     me = lax.axis_index("tile")
     q = lax.axis_index("mem")
@@ -177,18 +177,22 @@
 
     def y_first(dz):
         wait_for(group(q, dz), r_tile.at[dz])
-        go(remote(group(q, dz), group(q, dz), s_y.at[0, dz], r_y.at[0, dz], mem=at_y(1)))
-        go(remote(group(q, dz), group(q, dz), s_y.at[1, dz], r_y.at[1, dz], mem=at_y(-1)))
+        for late in range(2):
+            for i, to in enumerate((1, -1)):
+                h = (i + late) % 2
+                half = group(q, dz, 4 * h, 4)
+                go(remote(half, half, s_y.at[i, h, dz], r_y.at[i, h, dz], mem=at_y(to)))
 
     def y_second(i, dz):
         from_, to = ((-1, 1), (1, -1))[i]
-        wait_for(group(at_y(from_), dz), r_y.at[i, dz])
         half = group(at_y(from_), dz, 4 * i, 4)
-        go(remote(half, half, s_y.at[2 + i, dz], r_y2.at[i, dz], mem=at_y(to)))
+        wait_for(half, r_y.at[i, i, dz])
+        go(remote(half, half, s_y2.at[i, dz], r_y2.at[i, dz], mem=at_y(to)))
 
     def y_last(dz):
-        wait_for(group(at_y(2), dz, 0, 4), r_y2.at[0, dz])
-        wait_for(group(at_y(2), dz, 4, 4), r_y2.at[1, dz])
+        for i in range(2):
+            wait_for(group(at_y((-1, 1)[i]), dz, 4 - 4 * i, 4), r_y.at[i, 1 - i, dz])
+            wait_for(group(at_y(2), dz, 4 * i, 4), r_y2.at[i, dz])
 
     def block(oz, ox, own_core=True):
         return anoms.at[index(at_z(oz), at_x(ox), core if own_core else 1 - core)]
@@ -205,24 +209,27 @@
         b = block(oz, 0)
         src = b if src is None else src
         k = oz % NZ
-        go(remote(src, b, s_x.at[0, k], r_x.at[0, k], tile=index(z, at_x(1), core)))
-        go(remote(src, b, s_x.at[1, k], r_x.at[1, k], tile=index(z, at_x(-1), core)))
+        for late in range(2):
+            for i, to in enumerate((1, -1)):
+                h = (i + late) % 2
+                part = pl.ds(4 * h, 4)
+                go(remote(src.at[part], b.at[part], s_x.at[i, h, k], r_x.at[i, h, k], tile=index(z, at_x(to), core)))
         go(remote(src, b, s_sib.at[0, k], r_sib.at[0, k], tile=index(z, x, 1 - core)))
 
     def x_second(i, oz):
         k = oz % NZ
         from_, to = ((-1, 1), (1, -1))[i]
-        b = block(oz, from_)
-        wait_for(b, r_x.at[i, k])
-        h = b.at[pl.ds(4 * i, 4)]
-        go(remote(h, h, s_x.at[2 + i, k], r_x2.at[i, k], tile=index(z, at_x(to), core)))
-        to_sibling(oz, from_)
+        half = block(oz, from_).at[pl.ds(4 * i, 4)]
+        wait_for(half, r_x.at[i, i, k])
+        go(remote(half, half, s_x2.at[i, k], r_x2.at[i, k], tile=index(z, at_x(to), core)))
 
     def x_last(oz):
         k = oz % NZ
-        b = block(oz, 2)
-        wait_for(b.at[pl.ds(0, 4)], r_x2.at[0, k])
-        wait_for(b.at[pl.ds(4, 4)], r_x2.at[1, k])
+        for i, from_ in enumerate((-1, 1)):
+            wait_for(block(oz, from_).at[pl.ds(4 - 4 * i, 4)], r_x.at[i, 1 - i, k])
+            to_sibling(oz, from_)
+        for i in range(2):
+            wait_for(block(oz, 2).at[pl.ds(4 * i, 4)], r_x2.at[i, k])
         to_sibling(oz, 2)
 
     def z_step(i, k):
@@ -296,8 +303,8 @@
             pltpu.VMEM((NY, FLUX_DEV, B), F32),
             pltpu.VMEM((FLUX_DEV, LM, B), BF16),
             dma((3,)), dma, dma, dma((NY,)), dma((NY,)), dma, dma((NZ,)), dma, dma,
-            dma((4, NZ)), dma((2, NZ)), dma((2, NZ)),
-            dma, dma((2, 5)), dma((2, 5)), dma((4, NZ)), dma((2, NZ)), dma((2, NZ)),
+            dma((2, 2, NZ)), dma((2, 2, NZ)), dma((2, NZ)), dma((2, NZ)),
+            dma, dma((2, 5)), dma((2, 5)), dma((2, 2, NZ)), dma((2, 2, NZ)), dma((2, NZ)), dma((2, NZ)),
             dma((NX, NZ)), dma((NX, NZ)), pltpu.SemaphoreType.REGULAR((2, 5)),
         ],
         compiler_params=pltpu.CompilerParams(

time: 121 us -> 119 us (0.983)
  Pallas kernels: 119 us -> 117 us
    pallas_call x1, Pallas kernels: 71.2 us -> 69.7 us  [spread(): pl.pallas_call(spread_kernel, out_shape=(jax.ShapeDtypeStruct((NY, NT, CA...]
where the time goes in v6:
time: 119 us; the launch traced here: 118 us
  Pallas kernels  117 us (98%)
    pallas_call x1, Pallas kernels, spread(): pl.pallas_call(spread_kernel, out_shape=(jax.ShapeDtypeStruct((NY, NT, CA...  69.7 us
    pallas_call x1, Pallas kernels, gather(): pl.pallas_call(gather_kernel, out_shape=jax.ShapeDtypeStruct((LM, FLUX_DE...  37.6 us
    pallas_call x1, Pallas kernels, local(): pl.pallas_call(local_kernel, out_shape=jax.ShapeDtypeStruct((NT * FLUX_DE...  9.76 us

profile of v6, /device:TPU:8, one launch (start us, length us, event | category | flops | bytes accessed | tf_op | source)
XLA Modules:
  0.0 117.8 jit_solution(6600065333684045097)
XLA Ops:
  0.0 69.7 %spread.1 = (bf16[4,64,3,32,128]{4,3,2,1,0:T(8,128)(2,1)S(1)}, bf16[64,8,64,128]{3,2,1,0:T(8,128)(2,1)S(1)}, s32[64,1,128]{2,1,0:T(1,128)S(1)}) custom-call(s32[1,128]{1,0:T(1,128)} %bitcast.8, s32[1,128]{1,0:T(1,128)} %bitcast.9, bf16[128,128,128]{2,1,0:T(8,128)(2,1)} %footprints.1, bf16[64,1024]{1,0:T(8,128)(2,1)} %prior_h.1), custom_call_target="tpu_custom_call" | custom-call | tf_op jit(solution)/shard_map/spread/pallas_call | solution.py:285
  69.7 9.8 %local.1 = bf16[512,64,128]{2,1,0:T(8,128)(2,1)S(1)} custom-call(s32[64,1,128]{2,1,0:T(1,128)S(1)} %get-tuple-element.8.codes, bf16[4,64,3,32,128]{4,3,2,1,0:T(8,128)(2,1)S(1)} %get-tuple-element.9.tiles, bf16[512,64,128]{2,1,0:T(8,128)(2,1)S(1)} %bitcast.6, f32[64,2048]{1,0:T(8,128)} %observed_h.1, s32[16,1,128]{2,1,0:T(1,128)} %bitcast.7), custom_call_target="tpu_custom_call" | custom-call | tf_op jit(solution)/shard_map/local/pallas_call | solution.py:377
  79.5 37.6 %gather.1 = f32[64,1024]{1,0:T(8,128)S(1)} custom-call(bf16[8,4,2,8,64,128]{5,4,3,2,1,0:T(8,128)(2,1)S(1)} %bitcast.5), custom_call_target="tpu_custom_call" | custom-call | tf_op jit(solution)/shard_map/gather/pallas_call | solution.py:613
  117.1 0.7 copy.8

commit v7 on v6

--- a/solution.py
+++ b/solution.py
@@ -315,15 +315,23 @@
 
 
 def local_kernel(
-    codes, tiles, anoms, observed_h, weight_h, out,
-    observed, weight, modelled, weighted, total, s_obs, s_weight,
+    codes_v, tiles, anoms, observed_h, weight_h, out,
+    codes, s_codes, observed, weight, modelled, weighted, total, s_obs, s_weight,
 ):
+    codes_in = pltpu.make_async_copy(codes_v, codes, s_codes)
+    codes_in.start()
     observed_in = pltpu.make_async_copy(observed_h, observed, s_obs)
     observed_in.start()
     weight_in = pltpu.make_async_copy(weight_h, weight, s_weight)
     weight_in.start()
     modelled[...] = jnp.zeros_like(modelled)
-    step = 16
+
+    @pl.loop(0, NT)
+    def _(i):
+        total[pl.ds(i * 8, 8)] = jnp.zeros((8, LM, B), F32)
+
+    codes_in.wait()
+    step = 32
 
     def fetch(i, o, s):
         src = i * step + o
@@ -340,7 +348,6 @@
                     anoms[col], tile, (((1,), (1,)), ((), ())), preferred_element_type=F32
                 )
                 terms.append((row, term))
-        total[pl.ds(i * 128, 128)] = jnp.zeros((128, LM, B), F32)
         for row, term in terms:
             modelled[row] += term
 
@@ -377,9 +384,11 @@
     return pl.pallas_call(
         local_kernel,
         out_shape=jax.ShapeDtypeStruct((NT * FLUX_DEV, LM, B), BF16),
-        in_specs=[pl.BlockSpec(memory_space=pltpu.SMEM), vmem, vmem, hbm, hbm],
+        in_specs=[vmem, vmem, vmem, hbm, hbm],
         out_specs=vmem,
         scratch_shapes=[
+            pltpu.SMEM((NT, 1, B), jnp.int32),
+            dma,
             pltpu.VMEM((LM, SOUND_DEV * B), F32),
             pltpu.VMEM((SOUND_DEV, 1, B), jnp.int32),
             pltpu.VMEM((SOUND_DEV + 1, LM, B), F32),
@@ -398,6 +407,15 @@
 NEAR_X = (4, 5, 3, 6, 2, 7, 1, 0)
 FAR_Z = ((2, 1), (3, 0))
 NEAR_Z = (2, 1, 3, 0)
+
+GATHER_ORDER = (
+    ("b_far", 0), ("b_far", 1), ("a_far", 0), ("a_far", 1), ("a_far", 2), ("a_far", 3), ("b_near", 1, 0),
+    ("b_near", 1, 2), ("a_near", 0), ("b_near", 1, 1), ("b_near", 1, 3), ("a_near", 1), ("b_near", 2, 0),
+    ("b_near", 2, 2), ("a_near", 2), ("b_near", 2, 1), ("a_near", 3), ("b_near", 2, 3), ("b_near", 3, 0),
+    ("a_own", 4), ("a_near", 4), ("b_near", 3, 1), ("a_near", 5), ("b_near", 3, 2), ("b_own", 2),
+    ("a_own", 5), ("a_own", 3), ("a_near", 6), ("b_near", 3, 3), ("a_near", 7), ("a_own", 6), ("a_own", 2),
+    ("b_own", 3), ("b_own", 1), ("a_own", 7), ("a_own", 1), ("b_own", 0), ("a_own", 0),
+)
 
 
 def gather_kernel(
@@ -589,20 +607,11 @@
                 wait_for(xb2.at[i], r_xb.at[i, 1])
             result(NA, [*sources, xb2.at[0], xb2.at[1]], NB)
 
-    events = [(5.0, b_far, (k,)) for k in range(2)] + [(5.1, a_far, (k,)) for k in range(4)]
-    for j in range(8):
-        events.append((8.3 + 1.65 * (j // 2), a_near, (j,)))
-    for oz, when in ((4, 14.9), (5, 18.2), (3, 18.2), (6, 21.5), (2, 21.6), (7, 24.9), (1, 24.9), (0, 28.2)):
-        events.append((when, a_own, (oz,)))
-    for j in range(4):
-        for step, when in ((1, min(7.7 + j, 8.7)), (2, 10.4 + j), (3, 13.1 + j)):
-            events.append((when, b_near, (step, j)))
-    for ox, when in ((2, 18.6), (1, 23.0), (3, 23.1), (0, 28.5)):
-        events.append((when, b_own, (ox,)))
-    for _, act, args in sorted(events, key=lambda e: e[0]):
+    acts = {"a_far": a_far, "a_near": a_near, "a_own": a_own, "b_far": b_far, "b_near": b_near, "b_own": b_own}
+    for name, *numbers in GATHER_ORDER:
         while len(pending) > 30:
             pending.pop(0).wait_send()
-        act(*args)
+        acts[name](*numbers)
     for cp in pending:
         cp.wait_send()
 

time: 119 us -> 116 us (0.975)
  Pallas kernels: 117 us -> 115 us
    pallas_call x1, Pallas kernels: 37.6 us -> 36.4 us  [gather(): pl.pallas_call(gather_kernel, out_shape=jax.ShapeDtypeStruct((LM, FLUX_DE...]
where the time goes in v7:
time: 116 us
  Pallas kernels  115 us (99%)
    pallas_call x1, Pallas kernels, spread(): pl.pallas_call(spread_kernel, out_shape=(jax.ShapeDtypeStruct((NY, NT, CA...  69.7 us
    pallas_call x1, Pallas kernels, gather(): pl.pallas_call(gather_kernel, out_shape=jax.ShapeDtypeStruct((LM, FLUX_DE...  36.4 us
    pallas_call x1, Pallas kernels, local(): pl.pallas_call(local_kernel, out_shape=jax.ShapeDtypeStruct((NT * FLUX_DE...  8.88 us

profile of v7, /device:TPU:8, one launch (start us, length us, event | category | flops | bytes accessed | tf_op | source)
XLA Modules:
  0.0 115.7 jit_solution(4433623929319441318)
XLA Ops:
  0.0 69.7 %spread.1 = (bf16[4,64,3,32,128]{4,3,2,1,0:T(8,128)(2,1)S(1)}, bf16[64,8,64,128]{3,2,1,0:T(8,128)(2,1)S(1)}, s32[64,1,128]{2,1,0:T(1,128)S(1)}) custom-call(s32[1,128]{1,0:T(1,128)} %bitcast.8, s32[1,128]{1,0:T(1,128)} %bitcast.9, bf16[128,128,128]{2,1,0:T(8,128)(2,1)} %footprints.1, bf16[64,1024]{1,0:T(8,128)(2,1)} %prior_h.1), custom_call_target="tpu_custom_call" | custom-call | tf_op jit(solution)/shard_map/spread/pallas_call | solution.py:285
  69.7 8.9 %local.1 = bf16[512,64,128]{2,1,0:T(8,128)(2,1)S(1)} custom-call(s32[64,1,128]{2,1,0:T(1,128)S(1)} %get-tuple-element.8.codes_v, bf16[4,64,3,32,128]{4,3,2,1,0:T(8,128)(2,1)S(1)} %get-tuple-element.9.tiles, bf16[512,64,128]{2,1,0:T(8,128)(2,1)S(1)} %bitcast.6, f32[64,2048]{1,0:T(8,128)} %observed_h.1, s32[16,1,128]{2,1,0:T(1,128)} %bitcast.7), custom_call_target="tpu_custom_call" | custom-call | tf_op jit(solution)/shard_map/local/pallas_call | solution.py:384
  78.6 36.4 %gather.1 = f32[64,1024]{1,0:T(8,128)S(1)} custom-call(bf16[8,4,2,8,64,128]{5,4,3,2,1,0:T(8,128)(2,1)S(1)} %bitcast.5), custom_call_target="tpu_custom_call" | custom-call | tf_op jit(solution)/shard_map/gather/pallas_call | solution.py:622
  115.0 0.7 copy.8

commit v8 on v7

--- a/solution.py
+++ b/solution.py
@@ -372,9 +372,9 @@
         for col, term in terms:
             total[col] += term
 
-    @pl.loop(0, NT)
+    @pl.loop(0, NT // 4)
     def _(i):
-        out[pl.ds(i * 8, 8)] = total[pl.ds(i * 8, 8)].astype(BF16)
+        out[pl.ds(i * 32, 32)] = total[pl.ds(i * 32, 32)].astype(BF16)
 
 
 def local(codes, tiles, anoms, observed, weight):

time: 116 us -> 116 us (level)
  no operation moved by 1% of the time
where the time goes in v8:
time: 116 us; the launch traced here: 115 us
  Pallas kernels  115 us (99%)
    pallas_call x1, Pallas kernels, spread(): pl.pallas_call(spread_kernel, out_shape=(jax.ShapeDtypeStruct((NY, NT, CA...  69.7 us
    pallas_call x1, Pallas kernels, gather(): pl.pallas_call(gather_kernel, out_shape=jax.ShapeDtypeStruct((LM, FLUX_DE...  36.4 us
    pallas_call x1, Pallas kernels, local(): pl.pallas_call(local_kernel, out_shape=jax.ShapeDtypeStruct((NT * FLUX_DE...  8.65 us

profile of v8, /device:TPU:8, one launch (start us, length us, event | category | flops | bytes accessed | tf_op | source)
XLA Modules:
  0.0 115.5 jit_solution(11416495507867462297)
XLA Ops:
  0.0 69.7 %spread.1 = (bf16[4,64,3,32,128]{4,3,2,1,0:T(8,128)(2,1)S(1)}, bf16[64,8,64,128]{3,2,1,0:T(8,128)(2,1)S(1)}, s32[64,1,128]{2,1,0:T(1,128)S(1)}) custom-call(s32[1,128]{1,0:T(1,128)} %bitcast.8, s32[1,128]{1,0:T(1,128)} %bitcast.9, bf16[128,128,128]{2,1,0:T(8,128)(2,1)} %footprints.1, bf16[64,1024]{1,0:T(8,128)(2,1)} %prior_h.1), custom_call_target="tpu_custom_call" | custom-call | tf_op jit(solution)/shard_map/spread/pallas_call | solution.py:285
  69.7 8.6 %local.1 = bf16[512,64,128]{2,1,0:T(8,128)(2,1)S(1)} custom-call(s32[64,1,128]{2,1,0:T(1,128)S(1)} %get-tuple-element.8.codes_v, bf16[4,64,3,32,128]{4,3,2,1,0:T(8,128)(2,1)S(1)} %get-tuple-element.9.tiles, bf16[512,64,128]{2,1,0:T(8,128)(2,1)S(1)} %bitcast.6, f32[64,2048]{1,0:T(8,128)} %observed_h.1, s32[16,1,128]{2,1,0:T(1,128)} %bitcast.7), custom_call_target="tpu_custom_call" | custom-call | tf_op jit(solution)/shard_map/local/pallas_call | solution.py:384
  78.4 36.4 %gather.1 = f32[64,1024]{1,0:T(8,128)S(1)} custom-call(bf16[8,4,2,8,64,128]{5,4,3,2,1,0:T(8,128)(2,1)S(1)} %bitcast.5), custom_call_target="tpu_custom_call" | custom-call | tf_op jit(solution)/shard_map/gather/pallas_call | solution.py:622
  114.7 0.7 copy.8

commit v9 on v8

--- a/solution.py
+++ b/solution.py
@@ -43,14 +43,14 @@
 
 
 SPREAD_ORDER = (
-    ("T", 0), ("T", 1), ("T", 7), ("A0",), ("T", 2), ("T", 6), ("Y1", 0), ("Y1", 1), ("Y1", 7), ("Y2", 0, 0),
-    ("Y2", 1, 0), ("Z", 0, 1), ("X", 0, 0), ("X", 1, 0), ("Z", 1, 1), ("Y2", 0, 1), ("Y2", 1, 1), ("T", 3),
-    ("T", 5), ("X", 0, 7), ("X", 1, 7), ("Y2", 0, 7), ("Y2", 1, 7), ("Y1", 2), ("Y1", 6), ("XL", 0),
-    ("Z", 0, 2), ("X", 0, 1), ("X", 1, 1), ("Z", 1, 2), ("T", 4), ("XL", 7), ("Y2", 0, 2), ("Y2", 1, 2),
-    ("X", 0, 6), ("X", 1, 6), ("XL", 1), ("Y2", 0, 6), ("Y2", 1, 6), ("X", 0, 2), ("X", 1, 2), ("Y1", 3),
-    ("Y1", 5), ("Z", 0, 3), ("Z", 1, 3), ("XL", 6), ("XL", 2), ("Y2", 0, 3), ("Y2", 1, 3), ("X", 0, 5),
-    ("X", 1, 5), ("X", 0, 3), ("X", 1, 3), ("Y2", 0, 5), ("Y2", 1, 5), ("Y1", 4), ("Z", 0, 4), ("XL", 5),
-    ("XL", 3), ("X", 0, 4), ("X", 1, 4), ("Y2", 0, 4), ("Y2", 1, 4), ("XL", 4),
+    ("T", 0), ("T", 1), ("T", 7), ("A0",), ("T", 2), ("T", 6), ("Y1", 0), ("Y1", 1), ("Y2", 0, 0),
+    ("Y2", 1, 0), ("Z", 0, 1), ("X", 0, 0), ("X", 1, 0), ("Z", 1, 1), ("Y1", 7), ("Y2", 0, 1), ("Y2", 1, 1),
+    ("T", 3), ("T", 5), ("X", 0, 7), ("X", 1, 7), ("Y1", 2), ("XL", 0), ("Y2", 0, 7), ("Y2", 1, 7),
+    ("Z", 0, 2), ("X", 0, 1), ("X", 1, 1), ("Z", 1, 2), ("T", 4), ("Y1", 6), ("Y2", 0, 2), ("Y2", 1, 2),
+    ("XL", 7), ("X", 0, 6), ("X", 1, 6), ("XL", 1), ("Y2", 0, 6), ("Y2", 1, 6), ("X", 0, 2), ("X", 1, 2),
+    ("Y1", 3), ("Z", 0, 3), ("Z", 1, 3), ("Y1", 5), ("XL", 6), ("XL", 2), ("Y2", 0, 3), ("Y2", 1, 3),
+    ("X", 0, 5), ("X", 1, 5), ("X", 0, 3), ("X", 1, 3), ("Y2", 0, 5), ("Y2", 1, 5), ("Y1", 4), ("Z", 0, 4),
+    ("XL", 5), ("XL", 3), ("X", 0, 4), ("X", 1, 4), ("Y2", 0, 4), ("Y2", 1, 4), ("XL", 4),
 )
 
 

time: 116 us -> 115 us (level)
  no operation moved by 1% of the time
where the time goes in v9:
time: 115 us
  Pallas kernels  115 us (100%)
    pallas_call x1, Pallas kernels, spread(): pl.pallas_call(spread_kernel, out_shape=(jax.ShapeDtypeStruct((NY, NT, CA...  69.7 us
    pallas_call x1, Pallas kernels, gather(): pl.pallas_call(gather_kernel, out_shape=jax.ShapeDtypeStruct((LM, FLUX_DE...  36.1 us
    pallas_call x1, Pallas kernels, local(): pl.pallas_call(local_kernel, out_shape=jax.ShapeDtypeStruct((NT * FLUX_DE...  8.65 us

profile of v9, /device:TPU:8, one launch (start us, length us, event | category | flops | bytes accessed | tf_op | source)
XLA Modules:
  0.0 115.2 jit_solution(1786149345486823432)
XLA Ops:
  0.0 69.7 %spread.1 = (bf16[4,64,3,32,128]{4,3,2,1,0:T(8,128)(2,1)S(1)}, bf16[64,8,64,128]{3,2,1,0:T(8,128)(2,1)S(1)}, s32[64,1,128]{2,1,0:T(1,128)S(1)}) custom-call(s32[1,128]{1,0:T(1,128)} %bitcast.8, s32[1,128]{1,0:T(1,128)} %bitcast.9, bf16[128,128,128]{2,1,0:T(8,128)(2,1)} %footprints.1, bf16[64,1024]{1,0:T(8,128)(2,1)} %prior_h.1), custom_call_target="tpu_custom_call" | custom-call | tf_op jit(solution)/shard_map/spread/pallas_call | solution.py:285
  69.7 8.7 %local.1 = bf16[512,64,128]{2,1,0:T(8,128)(2,1)S(1)} custom-call(s32[64,1,128]{2,1,0:T(1,128)S(1)} %get-tuple-element.8.codes_v, bf16[4,64,3,32,128]{4,3,2,1,0:T(8,128)(2,1)S(1)} %get-tuple-element.9.tiles, bf16[512,64,128]{2,1,0:T(8,128)(2,1)S(1)} %bitcast.6, f32[64,2048]{1,0:T(8,128)} %observed_h.1, s32[16,1,128]{2,1,0:T(1,128)} %bitcast.7), custom_call_target="tpu_custom_call" | custom-call | tf_op jit(solution)/shard_map/local/pallas_call | solution.py:384
  78.4 36.1 %gather.1 = f32[64,1024]{1,0:T(8,128)S(1)} custom-call(bf16[8,4,2,8,64,128]{5,4,3,2,1,0:T(8,128)(2,1)S(1)} %bitcast.5), custom_call_target="tpu_custom_call" | custom-call | tf_op jit(solution)/shard_map/gather/pallas_call | solution.py:622
  114.5 0.7 copy.8

commit v10 on v9

--- a/solution.py
+++ b/solution.py
@@ -262,8 +262,6 @@
         "T": send_tiles, "A0": send_shard, "Z": z_step, "X": x_second, "XL": x_last, "Y1": y_first, "Y2": y_second
     }
     for name, *numbers in SPREAD_ORDER:
-        while len(pending) > 40:
-            pending.pop(0).wait_send()
         acts[name](*numbers)
     for dz in (0, 1, 7, 2, 6, 3, 5, 4):
         y_last(dz)

time: 115 us -> 116 us (level)
  no operation moved by 1% of the time
where the time goes in v10:
time: 116 us; the launch traced here: 115 us
  Pallas kernels  115 us (99%)
    pallas_call x1, Pallas kernels, spread(): pl.pallas_call(spread_kernel, out_shape=(jax.ShapeDtypeStruct((NY, NT, CA...  69.9 us
    pallas_call x1, Pallas kernels, gather(): pl.pallas_call(gather_kernel, out_shape=jax.ShapeDtypeStruct((LM, FLUX_DE...  36.1 us
    pallas_call x1, Pallas kernels, local(): pl.pallas_call(local_kernel, out_shape=jax.ShapeDtypeStruct((NT * FLUX_DE...  8.66 us

profile of v10, /device:TPU:8, one launch (start us, length us, event | category | flops | bytes accessed | tf_op | source)
XLA Modules:
  0.0 115.4 jit_solution(14814947828526068166)
XLA Ops:
  0.0 69.9 %spread.1 = (bf16[4,64,3,32,128]{4,3,2,1,0:T(8,128)(2,1)S(1)}, bf16[64,8,64,128]{3,2,1,0:T(8,128)(2,1)S(1)}, s32[64,1,128]{2,1,0:T(1,128)S(1)}) custom-call(s32[1,128]{1,0:T(1,128)} %bitcast.8, s32[1,128]{1,0:T(1,128)} %bitcast.9, bf16[128,128,128]{2,1,0:T(8,128)(2,1)} %footprints.1, bf16[64,1024]{1,0:T(8,128)(2,1)} %prior_h.1), custom_call_target="tpu_custom_call" | custom-call | tf_op jit(solution)/shard_map/spread/pallas_call | solution.py:283
  69.9 8.7 %local.1 = bf16[512,64,128]{2,1,0:T(8,128)(2,1)S(1)} custom-call(s32[64,1,128]{2,1,0:T(1,128)S(1)} %get-tuple-element.8.codes_v, bf16[4,64,3,32,128]{4,3,2,1,0:T(8,128)(2,1)S(1)} %get-tuple-element.9.tiles, bf16[512,64,128]{2,1,0:T(8,128)(2,1)S(1)} %bitcast.6, f32[64,2048]{1,0:T(8,128)} %observed_h.1, s32[16,1,128]{2,1,0:T(1,128)} %bitcast.7), custom_call_target="tpu_custom_call" | custom-call | tf_op jit(solution)/shard_map/local/pallas_call | solution.py:382
  78.5 36.1 %gather.1 = f32[64,1024]{1,0:T(8,128)S(1)} custom-call(bf16[8,4,2,8,64,128]{5,4,3,2,1,0:T(8,128)(2,1)S(1)} %bitcast.5), custom_call_target="tpu_custom_call" | custom-call | tf_op jit(solution)/shard_map/gather/pallas_call | solution.py:620
  114.7 0.7 copy.8
